TPU v7x, 512 devices: a whole 4x4x16 slice. The times are simulated.
512 devices in a mesh: firm: 32 (over x, y, z_hi), day: 16 (over z_lo, core).
Axes of the slice: x: 4, y: 4, z: 16 (z_hi: 2, z_lo: 8; z = z_hi * 8 + z_lo), core: 2. Of those that a mesh axis runs over, the one named last changes fastest.
Arguments:
- panel: float32 [65, 128, 16384], P(None, 'day', 'firm'), may hold values from -60 to 60, as said below
- presence: int32 [128, 16384], P(None, 'firm'), may hold values from 0 to 1, as said below
- firm_count: int32 [16384], P('firm'), may hold values from 1 to 128, as said below
- day_count: int32 [128], replicated, may hold values from 128 to 16384, as said below
Outputs:
- coefficients: float32 [64], replicated
- residual_panel: float32 [128, 16384], P('day', 'firm')
Inputs may be any that keep to these rules, and one draw needn't show every extreme that they name: presence is 0 or 1; every firm has at least one entry and every day at least 128 entries; some firm is present on every day and some day holds every firm; presence rates differ strongly across firms and days. firm_count is the number of ones of presence in that firm's column. day_count is the number of ones of presence in that day's row. `panel`: values at absent entries are arbitrary and are not used.
All inputs are finite; a program needn't handle non-finite values.
Results may differ from a plain program's by a relative error of at most 0.00025.
Values sent between devices are 32-bit elements; how exact they have to be, the bound alone decides.
No kernel may reach another device: no remote copies, remote signals or barrier semaphores. Data moves between devices by JAX's collectives and lax.ppermute only.
A program may use at most 64 MiB of HBM per device.

v0:
```python
import jax
import jax.numpy as jnp
from jax import lax
from jax.sharding import PartitionSpec as P

K = 64
SWEEPS = 3


def cross_products(block):
    flat = block.reshape(block.shape[0], -1)
    return jnp.dot(flat, flat.T, precision=lax.Precision.HIGHEST)


def firm_totals(current):
    return lax.psum(jnp.sum(current, axis=1), "day")


def axis_day_sum(day_part):
    return lax.psum(day_part, "firm")


def on_device(panel, presence, firm_count, day_count):
    cols, day_dev, firm_dev = panel.shape
    start = lax.axis_index("day") * day_dev
    mask_all = presence.astype(jnp.float32)
    mask_here = lax.dynamic_slice_in_dim(mask_all, start, day_dev, 0)
    firm_n = firm_count.astype(jnp.float32)
    day_all_n = day_count.astype(jnp.float32)
    day_here_n = lax.dynamic_slice_in_dim(day_all_n, start, day_dev, 0)
    current = panel * mask_here[None]
    gram = None
    for sweep in range(SWEEPS):
        firm_mean = firm_totals(current) / firm_n
        demeaned = mask_here[None] * (current - firm_mean[:, None, :])
        day_part = jnp.sum(demeaned, axis=2)
        day_mean = axis_day_sum(day_part) / day_here_n
        current = mask_here[None] * (demeaned - day_mean[:, :, None])
    gram = lax.psum(cross_products(current), ("firm", "day"))
    matrix = gram[:K, :K]
    target = gram[:K, K:]
    factor = jnp.linalg.cholesky(matrix)
    middle = lax.linalg.triangular_solve(factor, target, left_side=True, lower=True)
    coefficients = lax.linalg.triangular_solve(
        factor, middle, left_side=True, lower=True, transpose_a=True
    )[:, 0]
    fitted = jnp.tensordot(coefficients, current[:K], axes=1, precision=lax.Precision.HIGHEST)
    residual_panel = mask_here * (current[K] - fitted)
    return (coefficients, residual_panel)


def solution(mesh):
    placed = (P(None, "day", "firm"), P(None, "firm"), P("firm"), P())
    return jax.shard_map(
        on_device, mesh=mesh, in_specs=placed, out_specs=(P(), P("day", "firm")), check_vma=False
    )
```

profile of v0, /device:TPU:1, one launch (start us, length us, event | category | flops | bytes accessed | tf_op | source)
XLA Modules:
  0.0 1597.7 jit_solution(5766159034771134640)
XLA Ops:
  7.2 0.0 copy-start
  7.2 0.0 copy-start.3
  7.2 0.0 copy-start.2
  7.2 0.0 all-reduce.4.cloned.1.call-start
  7.2 0.8 dynamic-slice_convert_fusion
  8.0 2.2 multiply_reduce_fusion
  10.3 0.0 all-reduce.4.cloned.1.call-update
  10.3 0.0 all-reduce.6.cloned.1.call-start
  10.4 0.0 copy-done.3
  10.4 0.1 dynamic_slice.7
  10.5 0.0 copy-done.2
  10.5 192.5 %all-reduce.4.cloned.1.call-done = f32[65,512]{1,0:T(8,128)} async-done(((f32[65,512]{1,0:T(8,128)}), f32[65,512]{1,0:T(8,128)}) %all-reduce.4.cloned.1.call-update) | async-done | bytes 133136 | tf_op jit(solution)/shard_map/psum | solution.py:16
  203.0 0.9 broadcast_divide_fusion.2
  203.9 0.0 copy-done
  203.9 0.2 fusion.10
  204.1 274.4 %psum.50 = f32[65,8]{1,0:T(8,128)S(1)} all-reduce(f32[65,8]{1,0:T(8,128)S(1)} %fusion.10), channel_id=1, replica_groups=mesh['firm'=32,'day'=16] {'firm'}, use_global_device_ids=true, to_apply=%region_3.0 | all-reduce | flops 520 | bytes 4160 | tf_op jit(solution)/shard_map/psum | solution.py:20
  478.5 1.1 fusion.7
  479.7 0.0 all-reduce.6.cloned.1.call-update
  479.7 0.0 all-reduce.8.cloned.1.call-start
  479.7 205.2 %all-reduce.6.cloned.1.call-done = f32[65,512]{1,0:T(8,128)} async-done(((f32[65,512]{1,0:T(8,128)}), f32[65,512]{1,0:T(8,128)}) %all-reduce.6.cloned.1.call-update) | async-done | bytes 133136 | tf_op jit(solution)/shard_map/psum | solution.py:16
  684.9 0.9 broadcast_divide_fusion.1
  685.9 0.4 fusion.20
  686.3 274.4 %psum.52 = f32[65,8]{1,0:T(8,128)S(1)} all-reduce(f32[65,8]{1,0:T(8,128)S(1)} %fusion.20), channel_id=1, replica_groups=mesh['firm'=32,'day'=16] {'firm'}, use_global_device_ids=true, to_apply=%region_7.0 | all-reduce | flops 520 | bytes 4160 | tf_op jit(solution)/shard_map/psum | solution.py:20
  960.7 1.3 fusion.8
  962.0 0.0 all-reduce.8.cloned.1.call-update
  962.0 205.3 %all-reduce.8.cloned.1.call-done = f32[65,512]{1,0:T(8,128)} async-done(((f32[65,512]{1,0:T(8,128)}), f32[65,512]{1,0:T(8,128)}) %all-reduce.8.cloned.1.call-update) | async-done | bytes 133136 | tf_op jit(solution)/shard_map/psum | solution.py:16
  1167.3 0.9 broadcast_divide_fusion
  1168.2 0.7 fusion.9
  1168.9 274.3 %psum.54 = f32[65,8]{1,0:T(8,128)S(1)} all-reduce(f32[65,8]{1,0:T(8,128)S(1)} %fusion.9), channel_id=1, replica_groups=mesh['firm'=32,'day'=16] {'firm'}, use_global_device_ids=true, to_apply=%region_11.0 | all-reduce | flops 520 | bytes 4160 | tf_op jit(solution)/shard_map/psum | solution.py:20
  1443.2 0.5 subtract_multiply_fusion
  1443.7 2.2 fusion.2
  1445.9 0.1 slice.30
  1446.0 130.2 %psum.55 = f32[65,65]{0,1:T(8,128)S(1)} all-reduce(f32[65,65]{0,1:T(8,128)S(1)} %fusion.2), channel_id=1, replica_groups=mesh['firm'=32,'day'=16] {'firm','day'}, use_global_device_ids=true, to_apply=%region_12.0 | all-reduce | flops 4225 | bytes 33800 | tf_op jit(solution)/shard_map/psum | solution.py:39
  1576.2 0.1 copy.9
  1576.3 5.8 cholesky.16
  1582.1 0.6 compare_reduce_fusion
  1582.8 0.7 fusion.11
  1583.4 4.9 custom-call.8
  1588.3 0.2 convolution_bitcast_fusion
  1588.5 0.2 fusion.12
  1588.7 0.0 copy-start.1
  1588.7 1.2 fusion.5
  1589.8 1.3 fusion.17
  1591.2 0.0 copy-done.1
  (8 shorter events, 0.1 us)
Async XLA Ops:
  7.2 196.7 %copy-start = (f32[65,8,512]{2,1,0:T(8,128)S(1)}, f32[65,8,512]{2,1,0:T(8,128)}, u32[]{:S(2)}) copy-start(f32[65,8,512]{2,1,0:T(8,128)} %param.4) | copy-start | bytes 3194884
  7.2 3.2 copy-start.3
  7.2 3.3 copy-start.2
  7.2 195.8 %all-reduce.4.cloned.1.call-start = ((), (), s32[]{:S(2)}) async-start(), calls=%async_computation | async-start | bytes 294912 | tf_op jit(solution)/shard_map/psum | solution.py:16
  10.3 674.6 %all-reduce.6.cloned.1.call-start = ((), (), s32[]{:S(2)}) async-start(), calls=%async_computation.1 | async-start | bytes 294912 | tf_op jit(solution)/shard_map/psum | solution.py:16
  479.7 687.6 %all-reduce.8.cloned.1.call-start = ((), (), s32[]{:S(2)}) async-start(), calls=%async_computation.2 | async-start | bytes 294912 | tf_op jit(solution)/shard_map/psum | solution.py:16
  1588.7 2.5 copy-start.1
Sparse Core Ops, SparseCore 0:
  10.9 192.0 all-reduce.3
  479.8 205.0 all-reduce.5
  962.1 205.0 all-reduce.7
where the time goes:
time: 1600 us
  blocking collectives  953 us (60%)
  waiting for transfers between devices  603 us (38%)
  other arithmetic  23.5 us (1%)
    psum x3, blocking collectives, axis_day_sum(): return lax.psum(day_part, 'firm')  823 us
    psum x3, waiting for transfers between devices, firm_totals(): return lax.psum(jnp.sum(current, axis=1), 'day')  603 us
    psum x1, blocking collectives, on_device(): gram = lax.psum(cross_products(current), ('firm', 'day'))  130 us
  transfers between devices with their start and end apart: 3, of which 3 were waited for; matrix products, arithmetic and copies ran while one was open for 0% of the time, Pallas kernels for 0%

commit v1 on v0

v1 whole, which is shorter than its diff:
```python
import jax
import jax.numpy as jnp
from jax import lax
from jax.experimental import pallas as pl
from jax.experimental.pallas import tpu as pltpu
from jax.sharding import Mesh, PartitionSpec as P

K = 64
ROWS = 72
HIGHEST = lax.Precision.HIGHEST
F32 = jnp.float32


def iota(shape, axis):
    return lax.broadcasted_iota(jnp.int32, shape, axis)


def dot_t(a, b):
    return lax.dot_general(
        a, b, (((1,), (1,)), ((), ())), precision=HIGHEST, preferred_element_type=F32
    )


def dot(a, b):
    return lax.dot_general(
        a, b, (((1,), (0,)), ((), ())), precision=HIGHEST, preferred_element_type=F32
    )


def local_kernel(day_ref, panel_ref, pres_ref, msg_ref, gram_ref, rsum_ref):
    day = day_ref[0]
    mask = pres_ref[pl.ds(pl.multiple_of(day * 8, 8), 8), :].astype(F32)
    count = jnp.sum(mask, axis=0, keepdims=True)

    def column(t):
        tiles = []
        for j in range(4):
            target = panel_ref[32 * K + 8 * j + t : 32 * K + 8 * j + t + 1, :]
            regress = panel_ref[pl.ds(8 * j + t, K, stride=32), :]
            tiles.append(jnp.concatenate([regress, jnp.broadcast_to(target, (8, 128))], axis=0))
        return jnp.concatenate(tiles, axis=1)

    total = mask[0:1] * column(0)
    for t in range(1, 8):
        total = total + mask[t : t + 1] * column(t)
    for d in range(16):
        lanes = slice(32 * d, 32 * d + 32)
        msg_ref[d, 0:16, :] = jnp.concatenate(
            [total[16 * q : 16 * q + 16, lanes] for q in range(4)], axis=1
        )
        msg_ref[d, 16:24, :] = jnp.concatenate(
            [total[64:72, lanes], jnp.zeros((8, 96), F32)], axis=1
        )
    mean = total / jnp.maximum(count, 1.0)
    gram = jnp.zeros((ROWS, ROWS), F32)
    rsum = jnp.zeros((ROWS, 128), F32)
    lane = iota((ROWS, 128), 1)
    for t in range(8):
        centred = mask[t : t + 1] * (column(t) - mean)
        gram = gram + dot_t(centred, centred)
        sums = jnp.sum(centred, axis=1, keepdims=True)
        rsum = rsum + jnp.where(lane == 8 * day + t, sums, 0.0)
    gram_ref[...] = jnp.concatenate([gram, jnp.zeros((ROWS, 128 - ROWS), F32)], axis=1)
    rsum_ref[...] = rsum


def owner_kernel(day_ref, msg_ref, pres_ref, gram_ref, rsum_ref, pay_ref, mean_ref):
    day = day_ref[0]
    pick = (iota((512, 128), 0) == 32 * day + iota((512, 128), 1) % 32).astype(jnp.bfloat16)
    own = lax.dot_general(
        pres_ref[...].astype(F32).astype(jnp.bfloat16), pick, (((1,), (0,)), ((), ())),
        preferred_element_type=F32,
    )
    per_block = jnp.sum(own.reshape(16, 8, 128), axis=1)
    firm_n = jnp.sum(per_block, axis=0, keepdims=True)
    total = msg_ref[0]
    for b in range(1, 16):
        total = total + msg_ref[b]
    mean = total / firm_n
    delta = [msg_ref[b] / jnp.maximum(per_block[b : b + 1], 1.0) - mean for b in range(16)]

    def unpack(parts):
        rows = [
            jnp.concatenate([p[0:16, 32 * q : 32 * q + 32] for p in parts], axis=1)
            for q in range(4)
        ]
        rows.append(jnp.concatenate([p[16:24, 0:32] for p in parts], axis=1))
        return jnp.concatenate(rows, axis=0)

    mean_ref[...] = unpack([mean] * 4)
    gram = gram_ref[:, 0:ROWS]
    rsum = rsum_ref[...]
    block = iota((128, 128), 0) // 8
    group = iota((128, 128), 1) // 32
    for j in range(4):
        spread = unpack(delta[4 * j : 4 * j + 4])
        cells = jnp.where(block == 4 * j + group, own, 0.0)
        weight = jnp.sum(cells, axis=0, keepdims=True)
        gram = gram + dot_t(spread * weight, spread)
        rsum = rsum + dot_t(spread, cells)
    weight = jnp.where(iota((1, 128), 1) < 32, 1.0 / firm_n, 0.0)
    pay_ref[128:256, :] = dot_t(own * weight, own)
    pay_ref[0:64, :] = rsum[0:64]
    ret = rsum[64:72]
    row = iota((8, 128), 0)
    extra = jnp.where(
        row == 0,
        pltpu.roll(ret, 65, 1),
        jnp.where(row == 1, pltpu.roll(ret, 2, 1), jnp.where(row == 2, pltpu.roll(ret, 67, 1), 0.0)),
    )
    wide = jnp.concatenate([gram[0:64], jnp.zeros((64, 128 - ROWS), F32)], axis=1)
    extra = jnp.concatenate([extra, jnp.zeros((56, 128), F32)], axis=0)
    pay_ref[64:128, :] = jnp.where(iota((64, 128), 1) < 65, wide, extra)


def solve_kernel(day_ref, pay_ref, dayn_ref, mean_ref, w_ref, days_ref, firm_ref):
    day = day_ref[0]
    head = pay_ref[64:72, :]
    lane8 = iota((8, 128), 1)
    ret = jnp.where(
        lane8[0:1] < 63,
        pltpu.roll(head, 63, 1)[0:1],
        jnp.where(lane8[0:1] < 126, pltpu.roll(head, 126, 1)[1:2], pltpu.roll(head, 61, 1)[2:3]),
    )
    r = jnp.concatenate([pay_ref[0:64, :], jnp.broadcast_to(ret, (8, 128))], axis=0)
    cross = pay_ref[128:256, :]
    n = dayn_ref[...].astype(F32)
    d1 = r / n
    q1 = dot(d1, cross)
    d2 = q1 / n
    q2 = dot(d2, cross)
    d3 = q2 / n
    taken = dot_t(
        jnp.concatenate([r, q1, q2], axis=1), jnp.concatenate([d1 + d2, d2 + d3, d3], axis=1)
    )
    a = pay_ref[64:128, 0:ROWS] - taken[0:64, :]
    rowid = iota((64, ROWS), 0)
    for k in range(K):
        scaled = a[k : k + 1, :] / a[k : k + 1, k : k + 1]
        a = jnp.where(rowid == k, scaled, a - a[:, k : k + 1] * scaled)
    coef = a[:, 64:65]
    w = jnp.concatenate([-coef, (iota((8, 1), 0) == 0).astype(F32)], axis=0)
    w_ref[...] = jnp.sum(
        jnp.where(iota((ROWS, 128), 0) == iota((ROWS, 128), 1), w, 0.0), axis=0, keepdims=True
    )
    e = d1 + d2
    ew = jnp.sum(w * e, axis=0, keepdims=True)
    dw = jnp.sum(w * (e + d3), axis=0, keepdims=True)
    days_ref[...] = jnp.concatenate([ew, dw, jnp.zeros((6, 128), F32)], axis=0)
    fw = jnp.sum(w * mean_ref[...], axis=0, keepdims=True)
    firm_ref[...] = jnp.where(lane8[0:1] // 32 == day % 4, fw, 0.0)


def residual_kernel(day_ref, w_ref, panel_ref, pres_ref, firmn_ref, days_ref, firm_ref, out_ref):
    day = day_ref[0]
    mask = pres_ref[pl.ds(pl.multiple_of(day * 8, 8), 8), :].astype(F32)
    acc = panel_ref[32 * K : 32 * K + 32, :]
    for c in range(K):
        acc = acc + w_ref[0, c] * panel_ref[32 * c : 32 * c + 32, :]
    acc = jnp.concatenate([acc[8 * j : 8 * j + 8] for j in range(4)], axis=1)
    firm = jnp.concatenate(
        [jnp.sum(firm_ref[4 * j : 4 * j + 4, :], axis=0, keepdims=True) for j in range(4)], axis=1
    )
    days = days_ref[...]
    back = dot(days, pres_ref[...].astype(F32))[0:1]
    firm = back / firmn_ref[...].astype(F32) - firm
    here = iota((8, 128), 1) == 8 * day + iota((8, 128), 0)
    dw = jnp.sum(jnp.where(here, days[1:2], 0.0), axis=1, keepdims=True)
    out_ref[...] = mask * (acc + firm - dw)


def call(kernel, out, smem, *args):
    spaces = [pltpu.SMEM if i < smem else pltpu.VMEM for i in range(len(args))]
    return pl.pallas_call(
        kernel,
        out_shape=[jax.ShapeDtypeStruct(s, F32) for s in out],
        in_specs=[pl.BlockSpec(memory_space=s) for s in spaces],
        out_specs=[pl.BlockSpec(memory_space=pltpu.VMEM) for _ in out],
        name=kernel.__name__,
    )(*args)


def exchange(x, axes):
    return lax.all_to_all(x, axes, 0, 0, tiled=True)


def on_device(panel, presence, firm_count, day_count):
    day = lax.axis_index(("z", "c")).astype(jnp.int32).reshape(1)
    panel = panel.reshape(65, 8, 4, 128).transpose(0, 2, 1, 3).reshape(65 * 32, 128)
    msg, gram, rsum = call(
        local_kernel, [(16, 24, 128), (ROWS, 128), (ROWS, 128)], 1, day, panel, presence
    )
    msg = exchange(msg, ("z", "c"))
    pay, mean = call(owner_kernel, [(256, 128), (ROWS, 128)], 1, day, msg, presence, gram, rsum)
    pay = exchange(pay.reshape(32, 8, 128), ("x", "y", "c"))
    pay = jnp.broadcast_to(jnp.sum(pay, axis=0)[None], (16, 8, 128))
    pay = exchange(pay, ("h", "z"))
    pay = jnp.broadcast_to(jnp.sum(pay, axis=0)[None], (32, 8, 128))
    pay = exchange(pay, ("x", "y", "c")).reshape(256, 128)
    w, days, firm = call(
        solve_kernel, [(1, 128), (8, 128), (1, 128)], 1, day, pay, day_count.reshape(1, 128), mean
    )
    firm = exchange(jnp.broadcast_to(firm[None], (16, 1, 128)), ("z", "c")).reshape(16, 128)
    (residual,) = call(
        residual_kernel, [(8, 512)], 2, day, w, panel, presence, firm_count.reshape(1, 512), days, firm
    )
    return -w[0, :K], residual


def solution(mesh):
    split = Mesh(mesh.devices.reshape(4, 4, 2, 8, 2), ("x", "y", "h", "z", "c"))
    firm, day = ("x", "y", "h"), ("z", "c")
    return jax.shard_map(
        on_device,
        mesh=split,
        in_specs=(P(None, day, firm), P(None, firm), P(firm), P()),
        out_specs=(P(), P(day, firm)),
        check_vma=False,
    )
```

time: 1600 us -> 109 us (0.07)
  blocking collectives: 953 us -> 75.8 us
  waiting for transfers between devices: 603 us -> 8.55 us
  other arithmetic: 23.5 us -> 1.23 us
  Pallas kernels: 0 us -> 16.7 us
    psum x4 -> x0, blocking collectives: 953 us -> none  [the longest x3 823 us: axis_day_sum(): return lax.psum(day_part, 'firm')]
    psum x3 -> x0, waiting for transfers between devices: 603 us -> none  [firm_totals(): return lax.psum(jnp.sum(current, axis=1), 'day')]
    all_to_all x0 -> x4, blocking collectives: none -> 75.8 us  [exchange(): return lax.all_to_all(x, axes, 0, 0, tiled=True)]
    pallas_call x0 -> x4, Pallas kernels: none -> 16.7 us  [call(): pl.pallas_call(kernel, out_shape=[jax.ShapeDtypeStruct(s, F32) for s in o...]
  transfers between devices with their start and end apart: 3 -> 1, of which waited for: 3 -> 1; matrix products, arithmetic and copies ran while one was open for 0% -> 1% of each run, Pallas kernels for 0% -> 0%
where the time goes in v1:
time: 109 us; the launch traced here: 108 us
  blocking collectives  75.8 us (70%)
  Pallas kernels  16.7 us (15%)
  waiting for transfers between devices  8.55 us (8%)
  starting transfers between devices  3.65 us (3%)
  local copies, waits for them, and re-layouts  1.86 us (2%)
  other arithmetic  1.23 us (1%)
    all_to_all x4, blocking collectives, exchange(): return lax.all_to_all(x, axes, 0, 0, tiled=True)  75.8 us
    pallas_call x4, Pallas kernels, call(): pl.pallas_call(kernel, out_shape=[jax.ShapeDtypeStruct(s, F32) for s in o...  16.7 us
    all_to_all x1, waiting for transfers between devices, exchange(): return lax.all_to_all(x, axes, 0, 0, tiled=True)  8.55 us
    all_to_all x1, starting transfers between devices, exchange(): return lax.all_to_all(x, axes, 0, 0, tiled=True)  3.65 us
  transfers between devices with their start and end apart: 1, of which 1 were waited for; matrix products, arithmetic and copies ran while one was open for 1% of the time, Pallas kernels for 0%

profile of v1, /device:TPU:1, one launch (start us, length us, event | category | flops | bytes accessed | tf_op | source)
XLA Modules:
  0.0 108.4 jit_solution(7212064725628888771)
XLA Ops:
  0.6 3.7 %local_kernel.1 = (f32[16,24,128]{2,1,0:T(8,128)}, f32[72,128]{1,0:T(8,128)}, f32[72,128]{1,0:T(8,128)}) custom-call(s32[1]{0:T(128)} %bitcast.day_ref, f32[2080,128]{1,0:T(8,128)} %bitcast.14, s32[128,512]{1,0:T(8,128)} %pres_ref.5), custom_call_target="tpu_custom_call" | custom-call | tf_op jit(solution)/shard_map/local_kernel/pallas_call | solution.py:174
  4.4 28.8 %all_to_all.25.msg_ref = f32[16,24,128]{2,1,0:T(8,128)} all-to-all(f32[16,24,128]{2,1,0:T(8,128)} %get-tuple-element.10), channel_id=1, replica_groups=mesh['x'=4,'y'=4,'h'=2,'z'=8,'c'=2] {'z','c'}, dimensions={0} | all-to-all | bytes 393216 | tf_op jit(solution)/shard_map/all_to_all | solution.py:184
  33.2 2.9 %owner_kernel.1 = (f32[256,128]{1,0:T(8,128)}, f32[72,128]{1,0:T(8,128)}) custom-call(s32[1]{0:T(128)} %bitcast.day_ref, f32[16,24,128]{2,1,0:T(8,128)} %all_to_all.25.msg_ref, s32[128,512]{1,0:T(8,128)} %pres_ref.5, f32[72,128]{1,0:T(8,128)} %get-tuple-element.11.gram_ref, f32[72,128]{1,0:T(8,128)} %get-tuple-element.12.rsum_ref), custom_call_target="tpu_custom_call" | custom-call | tf_op jit(solution)/shard_map/owner_kernel/pallas_call | solution.py:174
  36.1 14.9 %all_to_all.26 = f32[32,8,128]{2,1,0:T(8,128)S(1)} all-to-all(f32[32,8,128]{2,1,0:T(8,128)} %bitcast.17), channel_id=1, replica_groups=mesh['x'=4,'y'=4,'h'=2,'z'=8,'c'=2] {'x','y','c'}, dimensions={0} | all-to-all | bytes 262144 | tf_op jit(solution)/shard_map/all_to_all | solution.py:184
  51.1 18.8 %all_to_all.27 = f32[16,8,128]{2,1,0:T(8,128)S(1)} all-to-all(f32[16,8,128]{2,1,0:T(8,128)S(1)} %broadcast_in_dim.8), channel_id=1, replica_groups=mesh['x'=4,'y'=4,'h'=2,'z'=8,'c'=2] {'h','z'}, dimensions={0} | all-to-all | bytes 131072 | tf_op jit(solution)/shard_map/all_to_all | solution.py:184
  69.9 13.3 %all_to_all.28 = f32[32,8,128]{2,1,0:T(8,128)} all-to-all(f32[32,8,128]{2,1,0:T(8,128)S(1)} %broadcast_in_dim.9), channel_id=1, replica_groups=mesh['x'=4,'y'=4,'h'=2,'z'=8,'c'=2] {'x','y','c'}, dimensions={0} | all-to-all | bytes 262144 | tf_op jit(solution)/shard_map/all_to_all | solution.py:184
  83.2 7.8 %solve_kernel.1 = (f32[1,128]{1,0:T(1,128)}, f32[8,128]{1,0:T(8,128)}, f32[1,128]{1,0:T(1,128)}) custom-call(s32[1]{0:T(128)} %bitcast.day_ref, f32[256,128]{1,0:T(8,128)} %bitcast.16, s32[1,128]{1,0:T(1,128)} %bitcast.20, f32[72,128]{1,0:T(8,128)} %get-tuple-element.14.mean_ref), custom_call_target="tpu_custom_call" | custom-call | tf_op jit(solution)/shard_map/solve_kernel/pallas_call | solution.py:174
  91.0 1.3 %broadcast_in_dim.11 = f32[16,1,128]{2,1,0:T(1,128)} broadcast(f32[128]{0:T(128)} %bitcast.21), dimensions={2} | broadcast | bytes 8704 | tf_op jit(solution)/shard_map/broadcast_in_dim | solution.py:203
  92.2 3.7 %all-to-all-start.4 = ((f32[16,1,128]{2,1,0:T(1,128)}), f32[16,1,128]{2,1,0:T(1,128)S(1)}, u32[]{:S(2)}, u32[]{:S(2)}) async-start(f32[16,1,128]{2,1,0:T(1,128)} %broadcast_in_dim.11), calls=%async_computation.4 | async-start | bytes 16384 | tf_op jit(solution)/shard_map/all_to_all | solution.py:184
  95.9 1.2 %negate_bitcast_fusion = f32[64]{0:T(128)} fusion(f32[1,128]{1,0:T(1,128)} %get-tuple-element.15.w_ref), kind=kLoop, calls=%fused_computation | loop fusion | flops 64 | bytes 512 | tf_op jit(solution)/shard_map/neg | solution.py:207
  97.1 8.6 %all-to-all-done.4 = f32[16,1,128]{2,1,0:T(1,128)S(1)} async-done(((f32[16,1,128]{2,1,0:T(1,128)}), f32[16,1,128]{2,1,0:T(1,128)S(1)}, u32[]{:S(2)}, u32[]{:S(2)}) %all-to-all-start.4) | async-done | bytes 8224 | tf_op jit(solution)/shard_map/all_to_all | solution.py:184
  105.6 0.0 copy-start
  105.6 0.6 copy-done
  106.2 2.2 %residual_kernel.1 = f32[8,512]{1,0:T(8,128)} custom-call(s32[1]{0:T(128)} %bitcast.day_ref, f32[1,128]{1,0:T(1,128)} %get-tuple-element.15.w_ref, f32[2080,128]{1,0:T(8,128)} %bitcast.15, s32[128,512]{1,0:T(8,128)} %pres_ref.5, s32[1,512]{1,0:T(1,128)} %bitcast.19, f32[8,128]{1,0:T(8,128)} %get-tuple-element.16.days_ref, f32[16,128]{1,0:T(8,128)} %bitcast.18), custom_call_target="tpu_custom_call" | custom-call | tf_op jit(solution)/shard_map/residual_kernel/pallas_call | solution.py:174
  (4 shorter events, 0.1 us)
Async XLA Ops:
  92.2 13.4 %all-to-all-start.4 = ((f32[16,1,128]{2,1,0:T(1,128)}), f32[16,1,128]{2,1,0:T(1,128)S(1)}, u32[]{:S(2)}, u32[]{:S(2)}) async-start(f32[16,1,128]{2,1,0:T(1,128)} %broadcast_in_dim.11), calls=%async_computation.4 | async-start | bytes 16384 | tf_op jit(solution)/shard_map/all_to_all | solution.py:184
  105.6 0.6 copy-start

commit v2 on v1

v2 whole, which is shorter than its diff:
```python
import jax
import jax.numpy as jnp
from jax import lax
from jax.experimental import pallas as pl
from jax.experimental.pallas import tpu as pltpu
from jax.sharding import Mesh, PartitionSpec as P

K = 64
ROWS = 72
HIGHEST = lax.Precision.HIGHEST
F32 = jnp.float32


def iota(shape, axis):
    return lax.broadcasted_iota(jnp.int32, shape, axis)


def dot_t(a, b):
    return lax.dot_general(
        a, b, (((1,), (1,)), ((), ())), precision=HIGHEST, preferred_element_type=F32
    )


def dot(a, b):
    return lax.dot_general(
        a, b, (((1,), (0,)), ((), ())), precision=HIGHEST, preferred_element_type=F32
    )


def stacked(panel_ref, t):
    tiles = []
    for j in range(4):
        row = 8 * j + t
        target = panel_ref[32 * K + row : 32 * K + row + 1, :]
        regress = panel_ref[pl.ds(row, K, stride=32), :]
        tiles.append(jnp.concatenate([regress, jnp.broadcast_to(target, (8, 128))], axis=0))
    return jnp.concatenate(tiles, axis=1)


def sums_kernel(day_ref, panel_hbm, pres_hbm, msg_ref, panel_ref, pres_ref, sems):
    start = pl.multiple_of(day_ref[0] * 8, 8)
    copies = [pltpu.make_async_copy(pres_hbm.at[pl.ds(start, 8), :], pres_ref, sems.at[0])]
    pieces = [slice(512 * q, 512 * q + 512) for q in range(4)] + [slice(32 * K, 32 * K + 32)]
    for i, rows in enumerate(pieces):
        copies.append(
            pltpu.make_async_copy(panel_hbm.at[rows, :], panel_ref.at[rows, :], sems.at[i + 1])
        )
    for copy in copies:
        copy.start()
    copies[0].wait()
    mask = pres_ref[...].astype(F32)
    for q in range(4):
        copies[q + 1].wait()
        tiles = []
        for j in range(4):
            total = None
            for t in range(8):
                x = panel_ref[pl.ds(512 * q + 8 * j + t, 16, stride=32), :]
                x = x * mask[t : t + 1, 128 * j : 128 * j + 128]
                total = x if total is None else total + x
            tiles.append(total)
        for d in range(16):
            lanes = slice(32 * (d % 4), 32 * (d % 4) + 32)
            msg_ref[17 * d : 17 * d + 16, 32 * q : 32 * q + 32] = tiles[d // 4][:, lanes]
    copies[5].wait()
    for j in range(4):
        x = panel_ref[32 * K + 8 * j : 32 * K + 8 * j + 8, :] * mask[:, 128 * j : 128 * j + 128]
        total = jnp.sum(x, axis=0, keepdims=True)
        for s in range(4):
            d = 4 * j + s
            msg_ref[17 * d + 16 : 17 * d + 17, :] = jnp.zeros((1, 128), F32)
            msg_ref[17 * d + 16 : 17 * d + 17, 0:32] = total[:, 32 * s : 32 * s + 32]


def scatter_kernel(day_ref, panel_ref, pres_ref, gram_ref, rsum_ref, own_ref, cross_ref):
    day = day_ref[0]
    mask = pres_ref[pl.ds(pl.multiple_of(day * 8, 8), 8), :].astype(F32)
    count = jnp.sum(mask, axis=0, keepdims=True)
    total = mask[0:1] * stacked(panel_ref, 0)
    for t in range(1, 8):
        total = total + mask[t : t + 1] * stacked(panel_ref, t)
    mean = total / jnp.maximum(count, 1.0)
    gram = jnp.zeros((ROWS, ROWS), F32)
    rsum = jnp.zeros((ROWS, 128), F32)
    lane = iota((ROWS, 128), 1)
    for t in range(8):
        centred = mask[t : t + 1] * (stacked(panel_ref, t) - mean)
        gram = gram + dot_t(centred, centred)
        sums = jnp.sum(centred, axis=1, keepdims=True)
        rsum = rsum + jnp.where(lane == 8 * day + t, sums, 0.0)
    gram_ref[...] = jnp.concatenate([gram, jnp.zeros((ROWS, 128 - ROWS), F32)], axis=1)
    rsum_ref[...] = rsum
    pick = (iota((512, 128), 0) == 32 * day + iota((512, 128), 1) % 32).astype(jnp.bfloat16)
    own = lax.dot_general(
        pres_ref[...].astype(F32).astype(jnp.bfloat16), pick, (((1,), (0,)), ((), ())),
        preferred_element_type=F32,
    )
    own_ref[...] = own
    firm_n = jnp.sum(own, axis=0, keepdims=True)
    weight = jnp.where(iota((1, 128), 1) < 32, 1.0 / firm_n, 0.0)
    cross_ref[...] = dot_t(own * weight, own)


def owner_kernel(msg_ref, gram_ref, rsum_ref, own_ref, cross_ref, pay_ref, mean_ref):
    own = own_ref[...]
    per_block = jnp.sum(own.reshape(16, 8, 128), axis=1)
    firm_n = jnp.sum(per_block, axis=0, keepdims=True)
    msg = [msg_ref[17 * b : 17 * b + 16, :] for b in range(16)]
    last = jnp.concatenate([msg_ref[17 * b + 16 : 17 * b + 17, :] for b in range(16)], axis=0)
    total = msg[0]
    for b in range(1, 16):
        total = total + msg[b]
    mean = total / firm_n
    last_mean = jnp.sum(last, axis=0, keepdims=True) / firm_n
    mean_ref[0:16, :] = mean
    mean_ref[16:17, :] = last_mean
    held = jnp.maximum(per_block, 1.0)
    delta = [msg[b] / held[b : b + 1] - mean for b in range(16)]
    last = last / held - last_mean

    gram = gram_ref[:, 0:ROWS]
    rsum = rsum_ref[...]
    block = iota((128, 128), 0) // 8
    group = iota((128, 128), 1) // 32
    for j in range(4):
        rows = [
            jnp.concatenate([delta[4 * j + s][:, 32 * q : 32 * q + 32] for s in range(4)], axis=1)
            for q in range(4)
        ]
        ret = jnp.concatenate([last[4 * j + s : 4 * j + s + 1, 0:32] for s in range(4)], axis=1)
        rows.append(jnp.broadcast_to(ret, (8, 128)))
        spread = jnp.concatenate(rows, axis=0)
        cells = jnp.where(block == 4 * j + group, own, 0.0)
        weight = jnp.sum(cells, axis=0, keepdims=True)
        gram = gram + dot_t(spread * weight, spread)
        rsum = rsum + dot_t(spread, cells)
    pay_ref[128:256, :] = cross_ref[...]
    pay_ref[0:64, :] = rsum[0:64]
    ret = rsum[64:72]
    row = iota((8, 128), 0)
    extra = jnp.where(
        row == 0,
        pltpu.roll(ret, 65, 1),
        jnp.where(row == 1, pltpu.roll(ret, 2, 1), jnp.where(row == 2, pltpu.roll(ret, 67, 1), 0.0)),
    )
    wide = jnp.concatenate([gram[0:64], jnp.zeros((64, 128 - ROWS), F32)], axis=1)
    extra = jnp.concatenate([extra, jnp.zeros((56, 128), F32)], axis=0)
    pay_ref[64:128, :] = jnp.where(iota((64, 128), 1) < 65, wide, extra)


def eliminate(a):
    rowid = iota((64, 128), 0)
    for k in range(0, K, 4):
        cols = [jnp.broadcast_to(a[:, k + j : k + j + 1], (64, 128)) for j in range(4)]
        rows = [a[k + i : k + i + 1, :] for i in range(4)]
        block = [[cols[j][k + i : k + i + 1, :] for j in range(4)] for i in range(4)]
        for i in range(4):
            inverse = 1.0 / block[i][i]
            rows[i] = rows[i] * inverse
            for j in range(i + 1, 4):
                block[i][j] = block[i][j] * inverse
            for m in range(4):
                if m != i:
                    rows[m] = rows[m] - block[m][i] * rows[i]
                    for j in range(i + 1, 4):
                        block[m][j] = block[m][j] - block[m][i] * block[i][j]
        rest = a
        for i in range(4):
            rest = rest - cols[i] * rows[i]
        for i in range(4):
            rest = jnp.where(rowid == k + i, rows[i], rest)
        a = rest
    return a


def solve_kernel(
    day_ref, side_ref, panel_hbm, pay_ref, dayn_ref, near_ref, far_ref, pres_ref, firmn_ref,
    coef_ref, out_ref, panel_ref, w_ref, sem,
):
    copy = pltpu.make_async_copy(panel_hbm, panel_ref, sem)
    copy.start()
    day = day_ref[0]
    lane = iota((1, 128), 1)
    head = pay_ref[64:72, :]
    ret = jnp.where(
        lane < 63,
        pltpu.roll(head, 63, 1)[0:1],
        jnp.where(lane < 126, pltpu.roll(head, 126, 1)[1:2], pltpu.roll(head, 61, 1)[2:3]),
    )
    r = jnp.concatenate([pay_ref[0:64, :], jnp.broadcast_to(ret, (8, 128))], axis=0)
    cross = pay_ref[128:256, :]
    n = dayn_ref[...].astype(F32)
    d1 = r / n
    q1 = dot(d1, cross)
    d2 = q1 / n
    q2 = dot(d2, cross)
    d3 = q2 / n
    right = jnp.concatenate([d1 + d2, d2 + d3, d3], axis=1)
    right = jnp.concatenate([right, jnp.zeros((128 - ROWS, 384), F32)], axis=0)
    left = jnp.concatenate([r[0:64], q1[0:64], q2[0:64]], axis=1)
    solved = eliminate(pay_ref[64:128, :] - dot_t(left, right))
    coef = jnp.broadcast_to(solved[:, 64:65], (64, 128))
    picked = jnp.where(iota((64, 128), 0) == iota((64, 128), 1), coef, 0.0)
    coef_ref[...] = jnp.sum(picked, axis=0, keepdims=True)[:, 0:K]
    w = jnp.concatenate([-coef, (iota((8, 128), 0) == 0).astype(F32)], axis=0)
    w_ref[...] = w
    e = d1 + d2
    ew = jnp.sum(w * e, axis=0, keepdims=True)
    dw = jnp.sum(w * (e + d3), axis=0, keepdims=True)
    back = dot(jnp.broadcast_to(ew, (8, 128)), pres_ref[...].astype(F32))[0:1]
    here = iota((8, 128), 1) == 8 * day + iota((8, 128), 0)
    dw = jnp.sum(jnp.where(here, dw, 0.0), axis=1, keepdims=True)
    packed = jnp.zeros((16, 128), F32)
    for q in range(4):
        packed = jnp.where(iota((16, 128), 1) // 32 == q, w[16 * q : 16 * q + 16], packed)
    core = day % 2
    first = 25 * 8 * side_ref[0]

    def part(ref, z):
        row = first + 25 * z + 8
        one = jnp.sum(packed * ref[pl.ds(row, 16), :], axis=0, keepdims=True)
        return one + jnp.where(lane < 32, ref[pl.ds(row + 16, 1), :], 0.0)

    parts = []
    for z in range(8):
        mine, theirs = part(near_ref, z), part(far_ref, z)
        parts += [jnp.where(core == 0, mine, theirs), jnp.where(core == 0, theirs, mine)]
    parts = jnp.concatenate(parts, axis=0)
    parts = parts + pltpu.roll(parts, 32, 1)
    parts = parts + pltpu.roll(parts, 64, 1)
    parts = jnp.where(iota((16, 128), 1) // 32 == iota((16, 128), 0) % 4, parts, 0.0)
    firm = jnp.concatenate(
        [jnp.sum(parts[4 * j : 4 * j + 4], axis=0, keepdims=True) for j in range(4)], axis=1
    )
    firm = back / firmn_ref[...].astype(F32) - firm
    mask = pres_ref[pl.ds(pl.multiple_of(day * 8, 8), 8), :].astype(F32)
    copy.wait()
    acc = panel_ref[32 * K : 32 * K + 32, :]
    for c in range(K):
        weight = jnp.broadcast_to(w_ref[c : c + 1, :], (32, 128))
        acc = acc + weight * panel_ref[32 * c : 32 * c + 32, :]
    acc = jnp.concatenate([acc[8 * j : 8 * j + 8] for j in range(4)], axis=1)
    out_ref[...] = mask * (acc + firm - dw)


def call(kernel, out, spaces, scratch, *args):
    kinds = {"s": pltpu.SMEM, "v": pltpu.VMEM, "p": pltpu.VMEM, "h": pl.ANY}
    args = [
        pltpu.with_memory_space_constraint(a, pltpu.VMEM) if s == "v" else a
        for s, a in zip(spaces, args)
    ]
    return pl.pallas_call(
        kernel,
        out_shape=[pltpu.VMEM(s, F32) if v else jax.ShapeDtypeStruct(s, F32) for s, v in out],
        in_specs=[pl.BlockSpec(memory_space=kinds[s]) for s in spaces],
        out_specs=[pl.BlockSpec(memory_space=pltpu.VMEM) for _ in out],
        scratch_shapes=scratch,
        name=kernel.__name__,
    )(*args)


PANEL = pltpu.VMEM((65 * 32, 128), F32)


def sums(day, panel, presence):
    scratch = [PANEL, pltpu.VMEM((8, 512), jnp.int32), pltpu.SemaphoreType.DMA((6,))]
    return call(sums_kernel, [((272, 128), True)], "shh", scratch, day, panel, presence)[0]


def scatter(day, panel, presence):
    shapes = [((n, 128), True) for n in (ROWS, ROWS, 128, 128)]
    return call(scatter_kernel, shapes, "spp", [], day, panel, presence)


def owner(*args):
    return call(owner_kernel, [((256, 128), True), ((17, 128), True)], "vvvvv", [], *args)


def solve(day, side, panel, pay, day_n, near, far, presence, firm_n):
    scratch = [PANEL, pltpu.VMEM((ROWS, 128), F32), pltpu.SemaphoreType.DMA]
    return call(
        solve_kernel, [((1, K), False), ((8, 512), False)], "sshvpvvpp", scratch,
        day, side, panel, pay, day_n, near, far, presence, firm_n,
    )


def exchange(x, axes):
    return lax.all_to_all(x, axes, 0, 0, tiled=True)


def on_device(panel, presence, firm_count, day_count):
    day = lax.axis_index(("z", "c")).astype(jnp.int32).reshape(1)
    side = lax.axis_index("h").astype(jnp.int32).reshape(1)
    panel = panel.reshape(65, 8, 4, 128).transpose(0, 2, 1, 3).reshape(65 * 32, 128)
    msg = exchange(sums(day, panel, presence).reshape(16, 1, 17 * 128), ("z", "c"))
    here = scatter(day, panel, presence)
    pay, mean = owner(msg.reshape(272, 128), *here)
    pay = jnp.sum(exchange(pay.reshape(32, 8, 128), ("x", "y", "c")), axis=0)
    near = jnp.concatenate([pay.reshape(1, 1, 8 * 128), mean.reshape(1, 1, 17 * 128)], axis=2)
    near = exchange(jnp.broadcast_to(near, (16, 1, 25 * 128)), ("h", "z"))
    far = lax.ppermute(near, "c", ((0, 1), (1, 0)))
    pay = jnp.sum(near[:, 0, : 8 * 128], axis=0).reshape(8, 128)
    pay = exchange(jnp.broadcast_to(pay[None], (32, 8, 128)), ("x", "y", "c")).reshape(256, 128)
    near, far = near.reshape(400, 128), far.reshape(400, 128)
    coef, residual = solve(
        day, side, panel, pay, day_count.reshape(1, 128), near, far, presence,
        firm_count.reshape(1, 512),
    )
    return coef.reshape(K), residual


def solution(mesh):
    split = Mesh(mesh.devices.reshape(4, 4, 2, 8, 2), ("x", "y", "h", "z", "c"))
    firm, day = ("x", "y", "h"), ("z", "c")
    return jax.shard_map(
        on_device,
        mesh=split,
        in_specs=(P(None, day, firm), P(None, firm), P(firm), P()),
        out_specs=(P(), P(day, firm)),
        check_vma=False,
    )
```

time: 109 us -> 90.1 us (0.83)
  blocking collectives: 75.8 us -> 20.2 us
  starting transfers between devices: 3.65 us -> 30.7 us
  waiting for transfers between devices: 8.55 us -> 24.4 us
  Pallas kernels: 16.7 us -> 12.8 us
  other arithmetic: 1.23 us -> 0.12 us
  local copies, waits for them, and re-layouts: 1.86 us -> 0.76 us
    all_to_all x4 -> x1, blocking collectives: 75.8 us -> 20.2 us  [exchange(): return lax.all_to_all(x, axes, 0, 0, tiled=True)]
    all_to_all x1 -> x3, starting transfers between devices: 3.65 us -> 25 us  [exchange(): return lax.all_to_all(x, axes, 0, 0, tiled=True)]
    all_to_all x1 -> x3, waiting for transfers between devices: 8.55 us -> 24.4 us  [exchange(): return lax.all_to_all(x, axes, 0, 0, tiled=True)]
    ppermute x0 -> x1, starting transfers between devices: none -> 5.77 us  [on_device(): far = lax.ppermute(near, 'c', ((0, 1), (1, 0)))]
    pallas_call x4, Pallas kernels: 16.7 us -> 12.8 us  [call(): pl.pallas_call(kernel, out_shape=[pltpu.VMEM(s, F32) if v else jax.ShapeD...]
    neg x1 -> x0, other arithmetic: 1.18 us -> none  [on_device(): return (-w[0, :K], residual)]
  transfers between devices with their start and end apart: 1 -> 4, of which waited for: 1 -> 3; matrix products, arithmetic and copies ran while one was open for 1% -> 1% of each run, Pallas kernels for 0% -> 4%
where the time goes in v2:
time: 90.1 us; the launch traced here: 89.6 us
  starting transfers between devices  30.7 us (34%)
  waiting for transfers between devices  24.4 us (27%)
  blocking collectives  20.2 us (22%)
  Pallas kernels  12.8 us (14%)
    all_to_all x3, starting transfers between devices, exchange(): return lax.all_to_all(x, axes, 0, 0, tiled=True)  25 us
    all_to_all x3, waiting for transfers between devices, exchange(): return lax.all_to_all(x, axes, 0, 0, tiled=True)  24.4 us
    all_to_all x1, blocking collectives, exchange(): return lax.all_to_all(x, axes, 0, 0, tiled=True)  20.2 us
    pallas_call x4, Pallas kernels, call(): pl.pallas_call(kernel, out_shape=[pltpu.VMEM(s, F32) if v else jax.ShapeD...  12.8 us
    ppermute x1, starting transfers between devices, on_device(): far = lax.ppermute(near, 'c', ((0, 1), (1, 0)))  5.77 us
  transfers between devices with their start and end apart: 4, of which 3 were waited for; matrix products, arithmetic and copies ran while one was open for 1% of the time, Pallas kernels for 4%

profile of v2, /device:TPU:1, one launch (start us, length us, event | category | flops | bytes accessed | tf_op | source)
XLA Modules:
  0.0 89.6 jit_solution(7903768107497575749)
XLA Ops:
  0.6 2.6 %sums_kernel.1 = f32[272,128]{1,0:T(8,128)} custom-call(s32[1]{0:T(128)} %bitcast.day_ref, f32[2080,128]{1,0:T(8,128)} %bitcast.22, s32[128,512]{1,0:T(8,128)} %pres_ref.3), custom_call_target="tpu_custom_call" | custom-call | tf_op jit(solution)/shard_map/sums_kernel/pallas_call | solution.py:252
  3.3 14.0 %all-to-all-start = ((f32[16,1,2176]{2,1,0:T(1,128)}), f32[16,1,2176]{2,1,0:T(1,128)S(1)}, u32[]{:S(2)}, u32[]{:S(2)}) async-start(f32[16,1,2176]{2,1,0:T(1,128)} %bitcast.7), calls=%async_computation | async-start | bytes 278528 | tf_op jit(solution)/shard_map/all_to_all | solution.py:288
  17.3 3.2 %scatter_kernel.1 = (f32[72,128]{1,0:T(8,128)S(1)}, f32[72,128]{1,0:T(8,128)S(1)}, f32[128,128]{1,0:T(8,128)S(1)}, f32[128,128]{1,0:T(8,128)S(1)}) custom-call(s32[1]{0:T(128)} %bitcast.day_ref, f32[2080,128]{1,0:T(8,128)} %bitcast.23, s32[128,512]{1,0:T(8,128)} %pres_ref.3), custom_call_target="tpu_custom_call" | custom-call | tf_op jit(solution)/shard_map/scatter_kernel/pallas_call | solution.py:252
  20.5 9.0 %all-to-all-done = f32[16,1,2176]{2,1,0:T(1,128)S(1)} async-done(((f32[16,1,2176]{2,1,0:T(1,128)}), f32[16,1,2176]{2,1,0:T(1,128)S(1)}, u32[]{:S(2)}, u32[]{:S(2)}) %all-to-all-start) | async-done | bytes 139296 | tf_op jit(solution)/shard_map/all_to_all | solution.py:288
  29.6 1.6 %owner_kernel.1 = (f32[256,128]{1,0:T(8,128)}, f32[17,128]{1,0:T(8,128)S(1)}) custom-call(f32[272,128]{1,0:T(8,128)S(1)} %bitcast.19, f32[72,128]{1,0:T(8,128)S(1)} %get-tuple-element.10.gram_ref, f32[72,128]{1,0:T(8,128)S(1)} %get-tuple-element.11.rsum_ref, f32[128,128]{1,0:T(8,128)S(1)} %get-tuple-element.12.own_ref, ...), custom_call_target="tpu_custom_call" | custom-call | tf_op jit(solution)/shard_map/owner_kernel/pallas_call | solution.py:252
  31.1 7.3 %all-to-all-start.1 = ((f32[32,8,128]{2,1,0:T(8,128)}), f32[32,8,128]{2,1,0:T(8,128)S(1)}, u32[]{:S(2)}, u32[]{:S(2)}) async-start(f32[32,8,128]{2,1,0:T(8,128)} %bitcast.9), calls=%async_computation.1 | async-start | bytes 262144 | tf_op jit(solution)/shard_map/all_to_all | solution.py:288
  38.4 7.7 %all-to-all-done.1 = f32[32,8,128]{2,1,0:T(8,128)S(1)} async-done(((f32[32,8,128]{2,1,0:T(8,128)}), f32[32,8,128]{2,1,0:T(8,128)S(1)}, u32[]{:S(2)}, u32[]{:S(2)}) %all-to-all-start.1) | async-done | bytes 131104 | tf_op jit(solution)/shard_map/all_to_all | solution.py:288
  46.2 0.1 broadcast_in_dim.15
  46.3 20.2 %all_to_all.20 = f32[16,1,3200]{2,1,0:T(1,128)S(1)} all-to-all(f32[16,1,3200]{2,1,0:T(1,128)S(1)} %broadcast_in_dim.15), channel_id=1, replica_groups=mesh['x'=4,'y'=4,'h'=2,'z'=8,'c'=2] {'h','z'}, dimensions={0} | all-to-all | bytes 409600 | tf_op jit(solution)/shard_map/all_to_all | solution.py:288
  66.5 5.8 %collective-permute-start = (f32[16,1,3200]{2,1,0:T(1,128)S(1)}, f32[16,1,3200]{2,1,0:T(1,128)S(1)}, u32[]{:S(2)}, u32[]{:S(2)}) collective-permute-start(f32[16,1,3200]{2,1,0:T(1,128)S(1)} %all_to_all.20), channel_id=1, source_target_pairs={{0,1},{1,0},{2,3},{3,2},{4,5},{5,4},{6,7},{7,6},{8,9},{9,8},{10,11... | collective-permute-start | bytes 614408 | tf_op jit(solution)/shard_map/ppermute | solution.py:301
  72.3 0.6 broadcast_in_dim.17
  72.9 3.6 %all-to-all-start.3 = ((f32[32,8,128]{2,1,0:T(8,128)}), f32[32,8,128]{2,1,0:T(8,128)S(1)}, u32[]{:S(2)}, u32[]{:S(2)}) async-start(f32[32,8,128]{2,1,0:T(8,128)} %broadcast_in_dim.17), calls=%async_computation.3 | async-start | bytes 262144 | tf_op jit(solution)/shard_map/all_to_all | solution.py:288
  76.6 7.7 %all-to-all-done.3 = f32[32,8,128]{2,1,0:T(8,128)S(1)} async-done(((f32[32,8,128]{2,1,0:T(8,128)}), f32[32,8,128]{2,1,0:T(8,128)S(1)}, u32[]{:S(2)}, u32[]{:S(2)}) %all-to-all-start.3) | async-done | bytes 131104 | tf_op jit(solution)/shard_map/all_to_all | solution.py:288
  84.2 0.0 collective-permute-done
  84.2 5.4 %solve_kernel.1 = (f32[1,64]{1,0:T(1,128)}, f32[8,512]{1,0:T(8,128)}) custom-call(s32[1]{0:T(128)} %bitcast.day_ref, s32[1]{0:T(128)} %bitcast.1.side_ref, f32[2080,128]{1,0:T(8,128)} %bitcast.24, f32[256,128]{1,0:T(8,128)S(1)} %bitcast.20, s32[1,128]{1,0:T(1,128)} %bitcast.28, f32[400,128]{1,0:T(8,128)S(1)} %bitcast.18, f32[400,128]{1,0:T(8,128)S(1)} %bitcast.21, ...), custom_call_target="tpu_custom_call" | custom-call | tf_op jit(solution)/shard_map/solve_kernel/pallas_call | solution.py:252
  (4 shorter events, 0.1 us)
Async XLA Ops:
  3.3 26.3 %all-to-all-start = ((f32[16,1,2176]{2,1,0:T(1,128)}), f32[16,1,2176]{2,1,0:T(1,128)S(1)}, u32[]{:S(2)}, u32[]{:S(2)}) async-start(f32[16,1,2176]{2,1,0:T(1,128)} %bitcast.7), calls=%async_computation | async-start | bytes 278528 | tf_op jit(solution)/shard_map/all_to_all | solution.py:288
  31.1 15.0 %all-to-all-start.1 = ((f32[32,8,128]{2,1,0:T(8,128)}), f32[32,8,128]{2,1,0:T(8,128)S(1)}, u32[]{:S(2)}, u32[]{:S(2)}) async-start(f32[32,8,128]{2,1,0:T(8,128)} %bitcast.9), calls=%async_computation.1 | async-start | bytes 262144 | tf_op jit(solution)/shard_map/all_to_all | solution.py:288
  66.5 17.8 %collective-permute-start = (f32[16,1,3200]{2,1,0:T(1,128)S(1)}, f32[16,1,3200]{2,1,0:T(1,128)S(1)}, u32[]{:S(2)}, u32[]{:S(2)}) collective-permute-start(f32[16,1,3200]{2,1,0:T(1,128)S(1)} %all_to_all.20), channel_id=1, source_target_pairs={{0,1},{1,0},{2,3},{3,2},{4,5},{5,4},{6,7},{7,6},{8,9},{9,8},{10,11... | collective-permute-start | bytes 614408 | tf_op jit(solution)/shard_map/ppermute | solution.py:301
  72.9 11.3 %all-to-all-start.3 = ((f32[32,8,128]{2,1,0:T(8,128)}), f32[32,8,128]{2,1,0:T(8,128)S(1)}, u32[]{:S(2)}, u32[]{:S(2)}) async-start(f32[32,8,128]{2,1,0:T(8,128)} %broadcast_in_dim.17), calls=%async_computation.3 | async-start | bytes 262144 | tf_op jit(solution)/shard_map/all_to_all | solution.py:288

commit v3 on v2

--- a/solution.py
+++ b/solution.py
@@ -49,16 +49,24 @@
         copy.start()
     copies[0].wait()
     mask = pres_ref[...].astype(F32)
+    low = [iota((8, 128), 0) % (2 * n) < n for n in (4, 2, 1)]
     for q in range(4):
         copies[q + 1].wait()
         tiles = []
         for j in range(4):
-            total = None
-            for t in range(8):
-                x = panel_ref[pl.ds(512 * q + 8 * j + t, 16, stride=32), :]
-                x = x * mask[t : t + 1, 128 * j : 128 * j + 128]
-                total = x if total is None else total + x
-            tiles.append(total)
+            held = mask[:, 128 * j : 128 * j + 128]
+            halves = []
+            for half in range(2):
+                base = 512 * q + 256 * half + 8 * j
+                rows = [base + 32 * c for c in (0, 4, 2, 6, 1, 5, 3, 7)]
+                level = [panel_ref[r : r + 8, :] * held for r in rows]
+                for n, mine in zip((4, 2, 1), low):
+                    level = [
+                        jnp.where(mine, x + pltpu.roll(x, 8 - n, 0), y + pltpu.roll(y, n, 0))
+                        for x, y in zip(level[0::2], level[1::2])
+                    ]
+                halves.append(level[0])
+            tiles.append(jnp.concatenate(halves, axis=0))
         for d in range(16):
             lanes = slice(32 * (d % 4), 32 * (d % 4) + 32)
             msg_ref[17 * d : 17 * d + 16, 32 * q : 32 * q + 32] = tiles[d // 4][:, lanes]
@@ -72,9 +80,16 @@
             msg_ref[17 * d + 16 : 17 * d + 17, 0:32] = total[:, 32 * s : 32 * s + 32]
 
 
-def scatter_kernel(day_ref, panel_ref, pres_ref, gram_ref, rsum_ref, own_ref, cross_ref):
+def scatter_kernel(
+    day_ref, panel_ref, pres_ref, dayn_ref, gram_ref, rsum_ref, own_ref, cross_ref, mask_ref, count_ref
+):
     day = day_ref[0]
-    mask = pres_ref[pl.ds(pl.multiple_of(day * 8, 8), 8), :].astype(F32)
+    every = pres_ref[...].astype(F32)
+    mask_ref[...] = every
+    firm_n = jnp.sum(every, axis=0, keepdims=True)
+    day_n = jnp.concatenate([dayn_ref[...].astype(F32), jnp.zeros((1, 384), F32)], axis=1)
+    count_ref[...] = jnp.concatenate([firm_n, day_n, jnp.zeros((6, 512), F32)], axis=0)
+    mask = mask_ref[pl.ds(pl.multiple_of(day * 8, 8), 8), :]
     count = jnp.sum(mask, axis=0, keepdims=True)
     total = mask[0:1] * stacked(panel_ref, 0)
     for t in range(1, 8):
@@ -92,7 +107,7 @@
     rsum_ref[...] = rsum
     pick = (iota((512, 128), 0) == 32 * day + iota((512, 128), 1) % 32).astype(jnp.bfloat16)
     own = lax.dot_general(
-        pres_ref[...].astype(F32).astype(jnp.bfloat16), pick, (((1,), (0,)), ((), ())),
+        every.astype(jnp.bfloat16), pick, (((1,), (0,)), ((), ())),
         preferred_element_type=F32,
     )
     own_ref[...] = own
@@ -174,8 +189,8 @@
 
 
 def solve_kernel(
-    day_ref, side_ref, panel_hbm, pay_ref, dayn_ref, near_ref, far_ref, pres_ref, firmn_ref,
-    coef_ref, out_ref, panel_ref, w_ref, sem,
+    day_ref, side_ref, panel_hbm, pay_ref, near_ref, far_ref, mask_ref, count_ref, coef_ref,
+    out_ref, panel_ref, w_ref, sem,
 ):
     copy = pltpu.make_async_copy(panel_hbm, panel_ref, sem)
     copy.start()
@@ -189,7 +204,7 @@
     )
     r = jnp.concatenate([pay_ref[0:64, :], jnp.broadcast_to(ret, (8, 128))], axis=0)
     cross = pay_ref[128:256, :]
-    n = dayn_ref[...].astype(F32)
+    n = count_ref[1:2, 0:128]
     d1 = r / n
     q1 = dot(d1, cross)
     d2 = q1 / n
@@ -207,7 +222,7 @@
     e = d1 + d2
     ew = jnp.sum(w * e, axis=0, keepdims=True)
     dw = jnp.sum(w * (e + d3), axis=0, keepdims=True)
-    back = dot(jnp.broadcast_to(ew, (8, 128)), pres_ref[...].astype(F32))[0:1]
+    back = dot(jnp.broadcast_to(ew, (8, 128)), mask_ref[...])[0:1]
     here = iota((8, 128), 1) == 8 * day + iota((8, 128), 0)
     dw = jnp.sum(jnp.where(here, dw, 0.0), axis=1, keepdims=True)
     packed = jnp.zeros((16, 128), F32)
@@ -232,8 +247,8 @@
     firm = jnp.concatenate(
         [jnp.sum(parts[4 * j : 4 * j + 4], axis=0, keepdims=True) for j in range(4)], axis=1
     )
-    firm = back / firmn_ref[...].astype(F32) - firm
-    mask = pres_ref[pl.ds(pl.multiple_of(day * 8, 8), 8), :].astype(F32)
+    firm = back / count_ref[0:1, :] - firm
+    mask = mask_ref[pl.ds(pl.multiple_of(day * 8, 8), 8), :]
     copy.wait()
     acc = panel_ref[32 * K : 32 * K + 32, :]
     for c in range(K):
@@ -267,20 +282,20 @@
     return call(sums_kernel, [((272, 128), True)], "shh", scratch, day, panel, presence)[0]
 
 
-def scatter(day, panel, presence):
+def scatter(day, panel, presence, day_n):
     shapes = [((n, 128), True) for n in (ROWS, ROWS, 128, 128)]
-    return call(scatter_kernel, shapes, "spp", [], day, panel, presence)
+    shapes += [((128, 512), True), ((8, 512), True)]
+    return call(scatter_kernel, shapes, "sppp", [], day, panel, presence, day_n)
 
 
 def owner(*args):
     return call(owner_kernel, [((256, 128), True), ((17, 128), True)], "vvvvv", [], *args)
 
 
-def solve(day, side, panel, pay, day_n, near, far, presence, firm_n):
+def solve(*args):
     scratch = [PANEL, pltpu.VMEM((ROWS, 128), F32), pltpu.SemaphoreType.DMA]
     return call(
-        solve_kernel, [((1, K), False), ((8, 512), False)], "sshvpvvpp", scratch,
-        day, side, panel, pay, day_n, near, far, presence, firm_n,
+        solve_kernel, [((1, K), False), ((8, 512), False)], "sshvvvvv", scratch, *args
     )
 
 
@@ -293,7 +308,7 @@
     side = lax.axis_index("h").astype(jnp.int32).reshape(1)
     panel = panel.reshape(65, 8, 4, 128).transpose(0, 2, 1, 3).reshape(65 * 32, 128)
     msg = exchange(sums(day, panel, presence).reshape(16, 1, 17 * 128), ("z", "c"))
-    here = scatter(day, panel, presence)
+    *here, mask, count = scatter(day, panel, presence, day_count.reshape(1, 128))
     pay, mean = owner(msg.reshape(272, 128), *here)
     pay = jnp.sum(exchange(pay.reshape(32, 8, 128), ("x", "y", "c")), axis=0)
     near = jnp.concatenate([pay.reshape(1, 1, 8 * 128), mean.reshape(1, 1, 17 * 128)], axis=2)
@@ -302,10 +317,7 @@
     pay = jnp.sum(near[:, 0, : 8 * 128], axis=0).reshape(8, 128)
     pay = exchange(jnp.broadcast_to(pay[None], (32, 8, 128)), ("x", "y", "c")).reshape(256, 128)
     near, far = near.reshape(400, 128), far.reshape(400, 128)
-    coef, residual = solve(
-        day, side, panel, pay, day_count.reshape(1, 128), near, far, presence,
-        firm_count.reshape(1, 512),
-    )
+    coef, residual = solve(day, side, panel, pay, near, far, mask, count)
     return coef.reshape(K), residual
 
 

time: 90.1 us -> 88.8 us (0.986)
  Pallas kernels: 12.8 us -> 11.5 us
    pallas_call x4, Pallas kernels: 12.8 us -> 11.5 us  [call(): pl.pallas_call(kernel, out_shape=[pltpu.VMEM(s, F32) if v else jax.ShapeD...]
where the time goes in v3:
time: 88.8 us; the launch traced here: 88.3 us
  starting transfers between devices  30.7 us (35%)
  waiting for transfers between devices  24.3 us (27%)
  blocking collectives  20.2 us (23%)
  Pallas kernels  11.5 us (13%)
    all_to_all x3, starting transfers between devices, exchange(): return lax.all_to_all(x, axes, 0, 0, tiled=True)  25 us
    all_to_all x3, waiting for transfers between devices, exchange(): return lax.all_to_all(x, axes, 0, 0, tiled=True)  24.3 us
    all_to_all x1, blocking collectives, exchange(): return lax.all_to_all(x, axes, 0, 0, tiled=True)  20.2 us
    pallas_call x4, Pallas kernels, call(): pl.pallas_call(kernel, out_shape=[pltpu.VMEM(s, F32) if v else jax.ShapeD...  11.5 us
    ppermute x1, starting transfers between devices, on_device(): far = lax.ppermute(near, 'c', ((0, 1), (1, 0)))  5.77 us
  transfers between devices with their start and end apart: 4, of which 3 were waited for; matrix products, arithmetic and copies ran while one was open for 1% of the time, Pallas kernels for 4%

profile of v3, /device:TPU:1, one launch (start us, length us, event | category | flops | bytes accessed | tf_op | source)
XLA Modules:
  0.0 88.3 jit_solution(270202513005286655)
XLA Ops:
  0.6 2.3 %sums_kernel.1 = f32[272,128]{1,0:T(8,128)} custom-call(s32[1]{0:T(128)} %bitcast.day_ref, f32[2080,128]{1,0:T(8,128)} %bitcast.21, s32[128,512]{1,0:T(8,128)} %pres_ref.1), custom_call_target="tpu_custom_call" | custom-call | tf_op jit(solution)/shard_map/sums_kernel/pallas_call | solution.py:267
  2.9 14.0 %all-to-all-start = ((f32[16,1,2176]{2,1,0:T(1,128)}), f32[16,1,2176]{2,1,0:T(1,128)S(1)}, u32[]{:S(2)}, u32[]{:S(2)}) async-start(f32[16,1,2176]{2,1,0:T(1,128)} %bitcast.7), calls=%async_computation | async-start | bytes 278528 | tf_op jit(solution)/shard_map/all_to_all | solution.py:303
  16.9 3.3 %scatter_kernel.1 = (f32[72,128]{1,0:T(8,128)S(1)}, f32[72,128]{1,0:T(8,128)S(1)}, f32[128,128]{1,0:T(8,128)S(1)}, f32[128,128]{1,0:T(8,128)S(1)}, f32[128,512]{1,0:T(8,128)S(1)}, /*index=5*/f32[8,512]{1,0:T(8,128)S(1)}) custom-call(s32[1]{0:T(128)} %bitcast.day_ref, f32[2080,128]{1,0:T(8,128)} %bitcast.22, s32[128,512]{1,0:T(8,128)} %pres_ref.1, ...), custom_call_target="tpu_custom_call" | custom-call | tf_op jit(solution)/shard_map/scatter_kernel/pallas_call | solution.py:267
  20.2 9.0 %all-to-all-done = f32[16,1,2176]{2,1,0:T(1,128)S(1)} async-done(((f32[16,1,2176]{2,1,0:T(1,128)}), f32[16,1,2176]{2,1,0:T(1,128)S(1)}, u32[]{:S(2)}, u32[]{:S(2)}) %all-to-all-start) | async-done | bytes 139296 | tf_op jit(solution)/shard_map/all_to_all | solution.py:303
  29.2 1.6 %owner_kernel.1 = (f32[256,128]{1,0:T(8,128)}, f32[17,128]{1,0:T(8,128)S(1)}) custom-call(f32[272,128]{1,0:T(8,128)S(1)} %bitcast.18, f32[72,128]{1,0:T(8,128)S(1)} %get-tuple-element.12.gram_ref, f32[72,128]{1,0:T(8,128)S(1)} %get-tuple-element.13.rsum_ref, f32[128,128]{1,0:T(8,128)S(1)} %get-tuple-element.14.own_ref, ...), custom_call_target="tpu_custom_call" | custom-call | tf_op jit(solution)/shard_map/owner_kernel/pallas_call | solution.py:267
  30.8 7.3 %all-to-all-start.1 = ((f32[32,8,128]{2,1,0:T(8,128)}), f32[32,8,128]{2,1,0:T(8,128)S(1)}, u32[]{:S(2)}, u32[]{:S(2)}) async-start(f32[32,8,128]{2,1,0:T(8,128)} %bitcast.10), calls=%async_computation.1 | async-start | bytes 262144 | tf_op jit(solution)/shard_map/all_to_all | solution.py:303
  38.1 7.7 %all-to-all-done.1 = f32[32,8,128]{2,1,0:T(8,128)S(1)} async-done(((f32[32,8,128]{2,1,0:T(8,128)}), f32[32,8,128]{2,1,0:T(8,128)S(1)}, u32[]{:S(2)}, u32[]{:S(2)}) %all-to-all-start.1) | async-done | bytes 131104 | tf_op jit(solution)/shard_map/all_to_all | solution.py:303
  45.8 0.1 broadcast_in_dim.15
  45.9 20.2 %all_to_all.20 = f32[16,1,3200]{2,1,0:T(1,128)S(1)} all-to-all(f32[16,1,3200]{2,1,0:T(1,128)S(1)} %broadcast_in_dim.15), channel_id=1, replica_groups=mesh['x'=4,'y'=4,'h'=2,'z'=8,'c'=2] {'h','z'}, dimensions={0} | all-to-all | bytes 409600 | tf_op jit(solution)/shard_map/all_to_all | solution.py:303
  66.1 5.8 %collective-permute-start = (f32[16,1,3200]{2,1,0:T(1,128)S(1)}, f32[16,1,3200]{2,1,0:T(1,128)S(1)}, u32[]{:S(2)}, u32[]{:S(2)}) collective-permute-start(f32[16,1,3200]{2,1,0:T(1,128)S(1)} %all_to_all.20), channel_id=1, source_target_pairs={{0,1},{1,0},{2,3},{3,2},{4,5},{5,4},{6,7},{7,6},{8,9},{9,8},{10,11... | collective-permute-start | bytes 614408 | tf_op jit(solution)/shard_map/ppermute | solution.py:316
  71.9 0.6 broadcast_in_dim.17
  72.5 3.6 %all-to-all-start.3 = ((f32[32,8,128]{2,1,0:T(8,128)}), f32[32,8,128]{2,1,0:T(8,128)S(1)}, u32[]{:S(2)}, u32[]{:S(2)}) async-start(f32[32,8,128]{2,1,0:T(8,128)} %broadcast_in_dim.17), calls=%async_computation.3 | async-start | bytes 262144 | tf_op jit(solution)/shard_map/all_to_all | solution.py:303
  76.2 7.7 %all-to-all-done.3 = f32[32,8,128]{2,1,0:T(8,128)S(1)} async-done(((f32[32,8,128]{2,1,0:T(8,128)}), f32[32,8,128]{2,1,0:T(8,128)S(1)}, u32[]{:S(2)}, u32[]{:S(2)}) %all-to-all-start.3) | async-done | bytes 131104 | tf_op jit(solution)/shard_map/all_to_all | solution.py:303
  83.8 0.0 collective-permute-done
  83.8 4.4 %solve_kernel.1 = (f32[1,64]{1,0:T(1,128)}, f32[8,512]{1,0:T(8,128)}) custom-call(s32[1]{0:T(128)} %bitcast.day_ref, s32[1]{0:T(128)} %bitcast.1.side_ref, f32[2080,128]{1,0:T(8,128)} %bitcast.23, f32[256,128]{1,0:T(8,128)S(1)} %bitcast.19, f32[400,128]{1,0:T(8,128)S(1)} %bitcast.17, f32[400,128]{1,0:T(8,128)S(1)} %bitcast.20, ...), custom_call_target="tpu_custom_call" | custom-call | tf_op jit(solution)/shard_map/solve_kernel/pallas_call | solution.py:267
  (4 shorter events, 0.1 us)
Async XLA Ops:
  2.9 26.3 %all-to-all-start = ((f32[16,1,2176]{2,1,0:T(1,128)}), f32[16,1,2176]{2,1,0:T(1,128)S(1)}, u32[]{:S(2)}, u32[]{:S(2)}) async-start(f32[16,1,2176]{2,1,0:T(1,128)} %bitcast.7), calls=%async_computation | async-start | bytes 278528 | tf_op jit(solution)/shard_map/all_to_all | solution.py:303
  30.8 15.0 %all-to-all-start.1 = ((f32[32,8,128]{2,1,0:T(8,128)}), f32[32,8,128]{2,1,0:T(8,128)S(1)}, u32[]{:S(2)}, u32[]{:S(2)}) async-start(f32[32,8,128]{2,1,0:T(8,128)} %bitcast.10), calls=%async_computation.1 | async-start | bytes 262144 | tf_op jit(solution)/shard_map/all_to_all | solution.py:303
  66.1 17.8 %collective-permute-start = (f32[16,1,3200]{2,1,0:T(1,128)S(1)}, f32[16,1,3200]{2,1,0:T(1,128)S(1)}, u32[]{:S(2)}, u32[]{:S(2)}) collective-permute-start(f32[16,1,3200]{2,1,0:T(1,128)S(1)} %all_to_all.20), channel_id=1, source_target_pairs={{0,1},{1,0},{2,3},{3,2},{4,5},{5,4},{6,7},{7,6},{8,9},{9,8},{10,11... | collective-permute-start | bytes 614408 | tf_op jit(solution)/shard_map/ppermute | solution.py:316
  72.5 11.3 %all-to-all-start.3 = ((f32[32,8,128]{2,1,0:T(8,128)}), f32[32,8,128]{2,1,0:T(8,128)S(1)}, u32[]{:S(2)}, u32[]{:S(2)}) async-start(f32[32,8,128]{2,1,0:T(8,128)} %broadcast_in_dim.17), calls=%async_computation.3 | async-start | bytes 262144 | tf_op jit(solution)/shard_map/all_to_all | solution.py:303

commit v4 on v3

--- a/solution.py
+++ b/solution.py
@@ -4,6 +4,7 @@
 from jax.experimental import pallas as pl
 from jax.experimental.pallas import tpu as pltpu
 from jax.sharding import Mesh, PartitionSpec as P
+
 
 K = 64
 ROWS = 72
@@ -127,8 +128,9 @@
         total = total + msg[b]
     mean = total / firm_n
     last_mean = jnp.sum(last, axis=0, keepdims=True) / firm_n
-    mean_ref[0:16, :] = mean
-    mean_ref[16:17, :] = last_mean
+    for k in range(16):
+        mean_ref[:, 128 * k : 128 * k + 128] = mean[k : k + 1]
+    mean_ref[:, 2048:2176] = last_mean
     held = jnp.maximum(per_block, 1.0)
     delta = [msg[b] / held[b : b + 1] - mean for b in range(16)]
     last = last / held - last_mean
@@ -149,18 +151,21 @@
         weight = jnp.sum(cells, axis=0, keepdims=True)
         gram = gram + dot_t(spread * weight, spread)
         rsum = rsum + dot_t(spread, cells)
-    pay_ref[128:256, :] = cross_ref[...]
-    pay_ref[0:64, :] = rsum[0:64]
-    ret = rsum[64:72]
-    row = iota((8, 128), 0)
+    wide = jnp.concatenate([gram, jnp.zeros((ROWS, 128 - ROWS), F32)], axis=1)
+    ret, rhs, row = rsum[64:72], wide[64:72], iota((8, 128), 0)
     extra = jnp.where(
         row == 0,
-        pltpu.roll(ret, 65, 1),
-        jnp.where(row == 1, pltpu.roll(ret, 2, 1), jnp.where(row == 2, pltpu.roll(ret, 67, 1), 0.0)),
-    )
-    wide = jnp.concatenate([gram[0:64], jnp.zeros((64, 128 - ROWS), F32)], axis=1)
-    extra = jnp.concatenate([extra, jnp.zeros((56, 128), F32)], axis=0)
-    pay_ref[64:128, :] = jnp.where(iota((64, 128), 1) < 65, wide, extra)
+        ret,
+        jnp.where(row == 1, pltpu.roll(ret, 96, 1), jnp.where(row == 2, rhs, pltpu.roll(rhs, 96, 1))),
+    )
+    extra = jnp.concatenate([extra, jnp.zeros((24, 128), F32)], axis=0)
+    lane = iota((32, 128), 1)
+    pay_ref[0:64, :] = rsum[0:64]
+    pay_ref[64:128, :] = cross_ref[0:64, :]
+    pay_ref[128:160, :] = jnp.where(lane < 64, wide[0:32], cross_ref[64:96, :])
+    pay_ref[160:192, :] = jnp.where(
+        lane // 32 == 1, wide[32:64], jnp.where(lane // 32 == 3, cross_ref[96:128, :], extra)
+    )
 
 
 def eliminate(a):
@@ -196,14 +201,37 @@
     copy.start()
     day = day_ref[0]
     lane = iota((1, 128), 1)
-    head = pay_ref[64:72, :]
-    ret = jnp.where(
-        lane < 63,
-        pltpu.roll(head, 63, 1)[0:1],
-        jnp.where(lane < 126, pltpu.roll(head, 126, 1)[1:2], pltpu.roll(head, 61, 1)[2:3]),
-    )
+    head = pay_ref[160:168, :]
+    moved = pltpu.roll(head, 32, 1)
+    ret = jnp.where(lane // 32 % 2 == 0, head[0:1], moved[1:2])
+    rhs = jnp.where(lane < 32, head[2:3], moved[3:4])
     r = jnp.concatenate([pay_ref[0:64, :], jnp.broadcast_to(ret, (8, 128))], axis=0)
-    cross = pay_ref[128:256, :]
+    top, mid, low = pay_ref[64:128, :], pay_ref[128:160, :], pay_ref[160:192, :]
+    wide = iota((32, 128), 1)
+    upper = [
+        jnp.where(wide >= 64, top[0:32], jnp.where(wide >= 32, mid, 0.0)),
+        jnp.where(wide >= 64, top[32:64], 0.0),
+        jnp.where(
+            wide >= 96, mid, jnp.where((iota((32, 128), 0) == 0) & (wide < 64), rhs, 0.0)
+        ),
+        jnp.zeros((32, 128), F32),
+    ]
+    lower = jnp.concatenate(upper, axis=0).T
+    cross = jnp.concatenate(
+        [
+            top,
+            jnp.where(wide >= 64, mid, 0.0) + lower[64:96],
+            jnp.where(wide >= 96, low, 0.0) + lower[96:128],
+        ],
+        axis=0,
+    )
+    gram = jnp.concatenate(
+        [
+            jnp.where(wide < 64, mid, 0.0) + lower[0:32],
+            jnp.where(wide // 32 == 1, low, 0.0) + lower[32:64],
+        ],
+        axis=0,
+    )
     n = count_ref[1:2, 0:128]
     d1 = r / n
     q1 = dot(d1, cross)
@@ -213,7 +241,7 @@
     right = jnp.concatenate([d1 + d2, d2 + d3, d3], axis=1)
     right = jnp.concatenate([right, jnp.zeros((128 - ROWS, 384), F32)], axis=0)
     left = jnp.concatenate([r[0:64], q1[0:64], q2[0:64]], axis=1)
-    solved = eliminate(pay_ref[64:128, :] - dot_t(left, right))
+    solved = eliminate(gram - dot_t(left, right))
     coef = jnp.broadcast_to(solved[:, 64:65], (64, 128))
     picked = jnp.where(iota((64, 128), 0) == iota((64, 128), 1), coef, 0.0)
     coef_ref[...] = jnp.sum(picked, axis=0, keepdims=True)[:, 0:K]
@@ -229,10 +257,10 @@
     for q in range(4):
         packed = jnp.where(iota((16, 128), 1) // 32 == q, w[16 * q : 16 * q + 16], packed)
     core = day % 2
-    first = 25 * 8 * side_ref[0]
+    first = 23 * 8 * side_ref[0]
 
     def part(ref, z):
-        row = first + 25 * z + 8
+        row = first + 23 * z + 6
         one = jnp.sum(packed * ref[pl.ds(row, 16), :], axis=0, keepdims=True)
         return one + jnp.where(lane < 32, ref[pl.ds(row + 16, 1), :], 0.0)
 
@@ -270,7 +298,6 @@
         in_specs=[pl.BlockSpec(memory_space=kinds[s]) for s in spaces],
         out_specs=[pl.BlockSpec(memory_space=pltpu.VMEM) for _ in out],
         scratch_shapes=scratch,
-        name=kernel.__name__,
     )(*args)
 
 
@@ -289,7 +316,7 @@
 
 
 def owner(*args):
-    return call(owner_kernel, [((256, 128), True), ((17, 128), True)], "vvvvv", [], *args)
+    return call(owner_kernel, [((192, 128), True), ((1, 17 * 128), True)], "vvvvv", [], *args)
 
 
 def solve(*args):
@@ -310,13 +337,14 @@
     msg = exchange(sums(day, panel, presence).reshape(16, 1, 17 * 128), ("z", "c"))
     *here, mask, count = scatter(day, panel, presence, day_count.reshape(1, 128))
     pay, mean = owner(msg.reshape(272, 128), *here)
-    pay = jnp.sum(exchange(pay.reshape(32, 8, 128), ("x", "y", "c")), axis=0)
-    near = jnp.concatenate([pay.reshape(1, 1, 8 * 128), mean.reshape(1, 1, 17 * 128)], axis=2)
-    near = exchange(jnp.broadcast_to(near, (16, 1, 25 * 128)), ("h", "z"))
+    pay = jnp.sum(exchange(pay.reshape(32, 1, 6 * 128), ("x", "y", "c")), axis=0)
+    near = jnp.concatenate([pay, mean], axis=1).reshape(1, 1, 23 * 128)
+    near = exchange(jnp.broadcast_to(near, (16, 1, 23 * 128)), ("h", "z"))
+    pay = jnp.sum(near[:, :, : 6 * 128], axis=0)
     far = lax.ppermute(near, "c", ((0, 1), (1, 0)))
-    pay = jnp.sum(near[:, 0, : 8 * 128], axis=0).reshape(8, 128)
-    pay = exchange(jnp.broadcast_to(pay[None], (32, 8, 128)), ("x", "y", "c")).reshape(256, 128)
-    near, far = near.reshape(400, 128), far.reshape(400, 128)
+    pay = exchange(jnp.broadcast_to(pay[None], (32, 1, 6 * 128)), ("x", "y", "c"))
+    pay = pay.reshape(192, 128)
+    near, far = near.reshape(368, 128), far.reshape(368, 128)
     coef, residual = solve(day, side, panel, pay, near, far, mask, count)
     return coef.reshape(K), residual
 

time: 88.8 us -> 87.3 us (0.983)
  blocking collectives: 20.2 us -> 34.2 us
  waiting for transfers between devices: 24.3 us -> 16.4 us
  starting transfers between devices: 30.7 us -> 23.6 us
    all_to_all x1 -> x2, blocking collectives: 20.2 us -> 34.2 us  [exchange(): return lax.all_to_all(x, axes, 0, 0, tiled=True)]
    all_to_all x3 -> x2, waiting for transfers between devices: 24.3 us -> 16.4 us  [exchange(): return lax.all_to_all(x, axes, 0, 0, tiled=True)]
    all_to_all x3 -> x2, starting transfers between devices: 25 us -> 17.7 us  [exchange(): return lax.all_to_all(x, axes, 0, 0, tiled=True)]
  transfers between devices with their start and end apart: 4 -> 3, of which waited for: 3 -> 2; matrix products, arithmetic and copies ran while one was open for 1% -> 1% of each run, Pallas kernels for 4% -> 4%
where the time goes in v4:
time: 87.3 us; the launch traced here: 86.8 us
  blocking collectives  34.2 us (39%)
  starting transfers between devices  23.6 us (27%)
  waiting for transfers between devices  16.4 us (19%)
  Pallas kernels  11 us (13%)
    all_to_all x2, blocking collectives, exchange(): return lax.all_to_all(x, axes, 0, 0, tiled=True)  34.2 us
    all_to_all x2, starting transfers between devices, exchange(): return lax.all_to_all(x, axes, 0, 0, tiled=True)  17.7 us
    all_to_all x2, waiting for transfers between devices, exchange(): return lax.all_to_all(x, axes, 0, 0, tiled=True)  16.4 us
    pallas_call x4, Pallas kernels, call(): pl.pallas_call(kernel, out_shape=[pltpu.VMEM(s, F32) if v else jax.ShapeD...  11 us
    ppermute x1, starting transfers between devices, on_device(): far = lax.ppermute(near, 'c', ((0, 1), (1, 0)))  5.95 us
  transfers between devices with their start and end apart: 3, of which 2 were waited for; matrix products, arithmetic and copies ran while one was open for 1% of the time, Pallas kernels for 4%

profile of v4, /device:TPU:1, one launch (start us, length us, event | category | flops | bytes accessed | tf_op | source)
XLA Modules:
  0.0 86.8 jit_solution(15517417254567573149)
XLA Ops:
  0.6 2.3 %shard_map.50 = f32[272,128]{1,0:T(8,128)} custom-call(s32[1]{0:T(128)} %bitcast.day_ref, f32[2080,128]{1,0:T(8,128)} %bitcast.20, s32[128,512]{1,0:T(8,128)} %pres_ref.1), custom_call_target="tpu_custom_call" | custom-call | tf_op jit(solution)/shard_map/pallas_call | solution.py:295
  2.9 14.0 %all-to-all-start = ((f32[16,1,2176]{2,1,0:T(1,128)}), f32[16,1,2176]{2,1,0:T(1,128)S(1)}, u32[]{:S(2)}, u32[]{:S(2)}) async-start(f32[16,1,2176]{2,1,0:T(1,128)} %bitcast.7), calls=%async_computation | async-start | bytes 278528 | tf_op jit(solution)/shard_map/all_to_all | solution.py:330
  16.9 3.3 %shard_map.51 = (f32[72,128]{1,0:T(8,128)S(1)}, f32[72,128]{1,0:T(8,128)S(1)}, f32[128,128]{1,0:T(8,128)S(1)}, f32[128,128]{1,0:T(8,128)S(1)}, f32[128,512]{1,0:T(8,128)S(1)}, /*index=5*/f32[8,512]{1,0:T(8,128)S(1)}) custom-call(s32[1]{0:T(128)} %bitcast.day_ref, f32[2080,128]{1,0:T(8,128)} %bitcast.21, s32[128,512]{1,0:T(8,128)} %pres_ref.1, s32[1,128]{1,0:T(1,128)} %bitcast.23), custom_call_target="tpu_custom_call" | custom-call | tf_op jit(solution)/shard_map/pallas_call | solution.py:295
  20.2 9.0 %all-to-all-done = f32[16,1,2176]{2,1,0:T(1,128)S(1)} async-done(((f32[16,1,2176]{2,1,0:T(1,128)}), f32[16,1,2176]{2,1,0:T(1,128)S(1)}, u32[]{:S(2)}, u32[]{:S(2)}) %all-to-all-start) | async-done | bytes 139296 | tf_op jit(solution)/shard_map/all_to_all | solution.py:330
  29.2 1.0 %shard_map.52 = (f32[192,128]{1,0:T(8,128)S(1)}, f32[1,2176]{1,0:T(1,128)S(1)}) custom-call(f32[272,128]{1,0:T(8,128)S(1)} %bitcast.16, f32[72,128]{1,0:T(8,128)S(1)} %get-tuple-element.12.gram_ref, f32[72,128]{1,0:T(8,128)S(1)} %get-tuple-element.13.rsum_ref, f32[128,128]{1,0:T(8,128)S(1)} %get-tuple-element.14.own_ref, ...), custom_call_target="tpu_custom_call" | custom-call | tf_op jit(solution)/shard_map/pallas_call | solution.py:295
  30.1 14.5 %all_to_all.20 = f32[32,1,768]{2,1,0:T(1,128)S(1)} all-to-all(f32[32,1,768]{2,1,0:T(1,128)S(1)} %bitcast.19), channel_id=1, replica_groups=mesh['x'=4,'y'=4,'h'=2,'z'=8,'c'=2] {'x','y','c'}, dimensions={0} | all-to-all | bytes 196608 | tf_op jit(solution)/shard_map/all_to_all | solution.py:330
  44.7 0.1 reduce_sum.20
  44.8 0.1 broadcast_in_dim.14
  44.9 19.6 %all_to_all.21 = f32[16,1,2944]{2,1,0:T(1,128)S(1)} all-to-all(f32[16,1,2944]{2,1,0:T(1,128)S(1)} %broadcast_in_dim.14), channel_id=1, replica_groups=mesh['x'=4,'y'=4,'h'=2,'z'=8,'c'=2] {'h','z'}, dimensions={0} | all-to-all | bytes 376832 | tf_op jit(solution)/shard_map/all_to_all | solution.py:330
  64.5 5.9 %collective-permute-start = (f32[16,1,2944]{2,1,0:T(1,128)S(1)}, f32[16,1,2944]{2,1,0:T(1,128)S(1)}, u32[]{:S(2)}, u32[]{:S(2)}) collective-permute-start(f32[16,1,2944]{2,1,0:T(1,128)S(1)} %all_to_all.21), channel_id=1, source_target_pairs={{0,1},{1,0},{2,3},{3,2},{4,5},{5,4},{6,7},{7,6},{8,9},{9,8},{10,11... | collective-permute-start | bytes 565256 | tf_op jit(solution)/shard_map/ppermute | solution.py:344
  70.5 0.7 broadcast_in_dim.15
  71.2 3.6 %all-to-all-start.3 = ((f32[32,1,768]{2,1,0:T(1,128)}), f32[32,1,768]{2,1,0:T(1,128)S(1)}, u32[]{:S(2)}, u32[]{:S(2)}) async-start(f32[32,1,768]{2,1,0:T(1,128)} %broadcast_in_dim.15), calls=%async_computation.3 | async-start | bytes 196608 | tf_op jit(solution)/shard_map/all_to_all | solution.py:330
  74.9 7.4 %all-to-all-done.3 = f32[32,1,768]{2,1,0:T(1,128)S(1)} async-done(((f32[32,1,768]{2,1,0:T(1,128)}), f32[32,1,768]{2,1,0:T(1,128)S(1)}, u32[]{:S(2)}, u32[]{:S(2)}) %all-to-all-start.3) | async-done | bytes 98336 | tf_op jit(solution)/shard_map/all_to_all | solution.py:330
  82.3 0.0 collective-permute-done
  82.3 4.5 %shard_map.53 = (f32[1,64]{1,0:T(1,128)}, f32[8,512]{1,0:T(8,128)}) custom-call(s32[1]{0:T(128)} %bitcast.day_ref, s32[1]{0:T(128)} %bitcast.1.side_ref, f32[2080,128]{1,0:T(8,128)} %bitcast.22, f32[192,128]{1,0:T(8,128)S(1)} %bitcast.17, f32[368,128]{1,0:T(8,128)S(1)} %bitcast.15, f32[368,128]{1,0:T(8,128)S(1)} %bitcast.18, ...), custom_call_target="tpu_custom_call" | custom-call | tf_op jit(solution)/shard_map/pallas_call | solution.py:295
  (3 shorter events, 0.1 us)
Async XLA Ops:
  2.9 26.3 %all-to-all-start = ((f32[16,1,2176]{2,1,0:T(1,128)}), f32[16,1,2176]{2,1,0:T(1,128)S(1)}, u32[]{:S(2)}, u32[]{:S(2)}) async-start(f32[16,1,2176]{2,1,0:T(1,128)} %bitcast.7), calls=%async_computation | async-start | bytes 278528 | tf_op jit(solution)/shard_map/all_to_all | solution.py:330
  64.5 17.8 %collective-permute-start = (f32[16,1,2944]{2,1,0:T(1,128)S(1)}, f32[16,1,2944]{2,1,0:T(1,128)S(1)}, u32[]{:S(2)}, u32[]{:S(2)}) collective-permute-start(f32[16,1,2944]{2,1,0:T(1,128)S(1)} %all_to_all.21), channel_id=1, source_target_pairs={{0,1},{1,0},{2,3},{3,2},{4,5},{5,4},{6,7},{7,6},{8,9},{9,8},{10,11... | collective-permute-start | bytes 565256 | tf_op jit(solution)/shard_map/ppermute | solution.py:344
  71.2 11.1 %all-to-all-start.3 = ((f32[32,1,768]{2,1,0:T(1,128)}), f32[32,1,768]{2,1,0:T(1,128)S(1)}, u32[]{:S(2)}, u32[]{:S(2)}) async-start(f32[32,1,768]{2,1,0:T(1,128)} %broadcast_in_dim.15), calls=%async_computation.3 | async-start | bytes 196608 | tf_op jit(solution)/shard_map/all_to_all | solution.py:330

commit v5 on v4

--- a/solution.py
+++ b/solution.py
@@ -26,6 +26,10 @@
     return lax.dot_general(
         a, b, (((1,), (0,)), ((), ())), precision=HIGHEST, preferred_element_type=F32
     )
+
+
+def day_index():
+    return lax.axis_index("z") * 2 + lax.axis_index("c")
 
 
 def stacked(panel_ref, t):
@@ -38,8 +42,8 @@
     return jnp.concatenate(tiles, axis=1)
 
 
-def sums_kernel(day_ref, panel_hbm, pres_hbm, msg_ref, panel_ref, pres_ref, sems):
-    start = pl.multiple_of(day_ref[0] * 8, 8)
+def sums_kernel(panel_hbm, pres_hbm, msg_ref, panel_ref, pres_ref, sems):
+    start = pl.multiple_of(day_index() * 8, 8)
     copies = [pltpu.make_async_copy(pres_hbm.at[pl.ds(start, 8), :], pres_ref, sems.at[0])]
     pieces = [slice(512 * q, 512 * q + 512) for q in range(4)] + [slice(32 * K, 32 * K + 32)]
     for i, rows in enumerate(pieces):
@@ -82,9 +86,9 @@
 
 
 def scatter_kernel(
-    day_ref, panel_ref, pres_ref, dayn_ref, gram_ref, rsum_ref, own_ref, cross_ref, mask_ref, count_ref
+    panel_ref, pres_ref, dayn_ref, gram_ref, rsum_ref, own_ref, cross_ref, mask_ref, count_ref
 ):
-    day = day_ref[0]
+    day = day_index()
     every = pres_ref[...].astype(F32)
     mask_ref[...] = every
     firm_n = jnp.sum(every, axis=0, keepdims=True)
@@ -194,12 +198,12 @@
 
 
 def solve_kernel(
-    day_ref, side_ref, panel_hbm, pay_ref, near_ref, far_ref, mask_ref, count_ref, coef_ref,
+    panel_hbm, pay_ref, near_ref, far_ref, mask_ref, count_ref, coef_ref,
     out_ref, panel_ref, w_ref, sem,
 ):
     copy = pltpu.make_async_copy(panel_hbm, panel_ref, sem)
     copy.start()
-    day = day_ref[0]
+    day = day_index()
     lane = iota((1, 128), 1)
     head = pay_ref[160:168, :]
     moved = pltpu.roll(head, 32, 1)
@@ -257,7 +261,7 @@
     for q in range(4):
         packed = jnp.where(iota((16, 128), 1) // 32 == q, w[16 * q : 16 * q + 16], packed)
     core = day % 2
-    first = 23 * 8 * side_ref[0]
+    first = 23 * 8 * lax.axis_index("h")
 
     def part(ref, z):
         row = first + 23 * z + 6
@@ -287,7 +291,7 @@
 
 
 def call(kernel, out, spaces, scratch, *args):
-    kinds = {"s": pltpu.SMEM, "v": pltpu.VMEM, "p": pltpu.VMEM, "h": pl.ANY}
+    kinds = {"v": pltpu.VMEM, "p": pltpu.VMEM, "h": pl.ANY}
     args = [
         pltpu.with_memory_space_constraint(a, pltpu.VMEM) if s == "v" else a
         for s, a in zip(spaces, args)
@@ -304,15 +308,15 @@
 PANEL = pltpu.VMEM((65 * 32, 128), F32)
 
 
-def sums(day, panel, presence):
+def sums(panel, presence):
     scratch = [PANEL, pltpu.VMEM((8, 512), jnp.int32), pltpu.SemaphoreType.DMA((6,))]
-    return call(sums_kernel, [((272, 128), True)], "shh", scratch, day, panel, presence)[0]
-
-
-def scatter(day, panel, presence, day_n):
+    return call(sums_kernel, [((272, 128), True)], "hh", scratch, panel, presence)[0]
+
+
+def scatter(panel, presence, day_n):
     shapes = [((n, 128), True) for n in (ROWS, ROWS, 128, 128)]
     shapes += [((128, 512), True), ((8, 512), True)]
-    return call(scatter_kernel, shapes, "sppp", [], day, panel, presence, day_n)
+    return call(scatter_kernel, shapes, "ppp", [], panel, presence, day_n)
 
 
 def owner(*args):
@@ -322,7 +326,7 @@
 def solve(*args):
     scratch = [PANEL, pltpu.VMEM((ROWS, 128), F32), pltpu.SemaphoreType.DMA]
     return call(
-        solve_kernel, [((1, K), False), ((8, 512), False)], "sshvvvvv", scratch, *args
+        solve_kernel, [((1, K), False), ((8, 512), False)], "hvvvvv", scratch, *args
     )
 
 
@@ -331,11 +335,9 @@
 
 
 def on_device(panel, presence, firm_count, day_count):
-    day = lax.axis_index(("z", "c")).astype(jnp.int32).reshape(1)
-    side = lax.axis_index("h").astype(jnp.int32).reshape(1)
     panel = panel.reshape(65, 8, 4, 128).transpose(0, 2, 1, 3).reshape(65 * 32, 128)
-    msg = exchange(sums(day, panel, presence).reshape(16, 1, 17 * 128), ("z", "c"))
-    *here, mask, count = scatter(day, panel, presence, day_count.reshape(1, 128))
+    msg = exchange(sums(panel, presence).reshape(16, 1, 17 * 128), ("z", "c"))
+    *here, mask, count = scatter(panel, presence, day_count.reshape(1, 128))
     pay, mean = owner(msg.reshape(272, 128), *here)
     pay = jnp.sum(exchange(pay.reshape(32, 1, 6 * 128), ("x", "y", "c")), axis=0)
     near = jnp.concatenate([pay, mean], axis=1).reshape(1, 1, 23 * 128)
@@ -345,7 +347,7 @@
     pay = exchange(jnp.broadcast_to(pay[None], (32, 1, 6 * 128)), ("x", "y", "c"))
     pay = pay.reshape(192, 128)
     near, far = near.reshape(368, 128), far.reshape(368, 128)
-    coef, residual = solve(day, side, panel, pay, near, far, mask, count)
+    coef, residual = solve(panel, pay, near, far, mask, count)
     return coef.reshape(K), residual
 
 

time: 87.3 us -> 87.3 us (level)
  blocking collectives: 34.2 us -> 44.9 us
  waiting for transfers between devices: 16.4 us -> 8.95 us
  starting transfers between devices: 23.6 us -> 20 us
  Pallas kernels: 11 us -> 12.1 us
    all_to_all x2 -> x3, blocking collectives: 34.2 us -> 44.9 us  [exchange(): return lax.all_to_all(x, axes, 0, 0, tiled=True)]
    all_to_all x2 -> x1, waiting for transfers between devices: 16.4 us -> 8.95 us  [exchange(): return lax.all_to_all(x, axes, 0, 0, tiled=True)]
    all_to_all x2 -> x1, starting transfers between devices: 17.7 us -> 14 us  [exchange(): return lax.all_to_all(x, axes, 0, 0, tiled=True)]
    pallas_call x4, Pallas kernels: 11 us -> 12.1 us  [call(): pl.pallas_call(kernel, out_shape=[pltpu.VMEM(s, F32) if v else jax.ShapeD...]
  transfers between devices with their start and end apart: 3 -> 2, of which waited for: 2 -> 1; matrix products, arithmetic and copies ran while one was open for 1% -> 0% of each run, Pallas kernels for 4% -> 4%
where the time goes in v5:
time: 87.3 us; the launch traced here: 86.9 us
  blocking collectives  44.9 us (51%)
  starting transfers between devices  20 us (23%)
  Pallas kernels  12.1 us (14%)
  waiting for transfers between devices  8.95 us (10%)
    all_to_all x3, blocking collectives, exchange(): return lax.all_to_all(x, axes, 0, 0, tiled=True)  44.9 us
    all_to_all x1, starting transfers between devices, exchange(): return lax.all_to_all(x, axes, 0, 0, tiled=True)  14 us
    pallas_call x4, Pallas kernels, call(): pl.pallas_call(kernel, out_shape=[pltpu.VMEM(s, F32) if v else jax.ShapeD...  12.1 us
    all_to_all x1, waiting for transfers between devices, exchange(): return lax.all_to_all(x, axes, 0, 0, tiled=True)  8.95 us
    ppermute x1, starting transfers between devices, on_device(): far = lax.ppermute(near, 'c', ((0, 1), (1, 0)))  5.95 us
  transfers between devices with their start and end apart: 2, of which 1 were waited for; matrix products, arithmetic and copies ran while one was open for 0% of the time, Pallas kernels for 4%

profile of v5, /device:TPU:1, one launch (start us, length us, event | category | flops | bytes accessed | tf_op | source)
XLA Modules:
  0.0 86.9 jit_solution(15157667474096174912)
XLA Ops:
  0.6 2.3 %shard_map.50 = f32[272,128]{1,0:T(8,128)} custom-call(f32[2080,128]{1,0:T(8,128)} %bitcast.18, s32[128,512]{1,0:T(8,128)} %pres_ref.1), custom_call_target="tpu_custom_call" | custom-call | tf_op jit(solution)/shard_map/pallas_call | solution.py:299
  2.9 14.0 %all-to-all-start = ((f32[16,1,2176]{2,1,0:T(1,128)}), f32[16,1,2176]{2,1,0:T(1,128)S(1)}, u32[]{:S(2)}, u32[]{:S(2)}) async-start(f32[16,1,2176]{2,1,0:T(1,128)} %bitcast.5), calls=%async_computation | async-start | bytes 278528 | tf_op jit(solution)/shard_map/all_to_all | solution.py:334
  16.9 3.3 %shard_map.51 = (f32[72,128]{1,0:T(8,128)S(1)}, f32[72,128]{1,0:T(8,128)S(1)}, f32[128,128]{1,0:T(8,128)S(1)}, f32[128,128]{1,0:T(8,128)S(1)}, f32[128,512]{1,0:T(8,128)S(1)}, /*index=5*/f32[8,512]{1,0:T(8,128)S(1)}) custom-call(f32[2080,128]{1,0:T(8,128)} %bitcast.19, s32[128,512]{1,0:T(8,128)} %pres_ref.1, s32[1,128]{1,0:T(1,128)} %bitcast.21), custom_call_target="tpu_custom_call" | custom-call | tf_op jit(solution)/shard_map/pallas_call | solution.py:299
  20.2 8.9 %all-to-all-done = f32[16,1,2176]{2,1,0:T(1,128)S(1)} async-done(((f32[16,1,2176]{2,1,0:T(1,128)}), f32[16,1,2176]{2,1,0:T(1,128)S(1)}, u32[]{:S(2)}, u32[]{:S(2)}) %all-to-all-start) | async-done | bytes 139296 | tf_op jit(solution)/shard_map/all_to_all | solution.py:334
  29.2 1.0 %shard_map.52 = (f32[192,128]{1,0:T(8,128)S(1)}, f32[1,2176]{1,0:T(1,128)S(1)}) custom-call(f32[272,128]{1,0:T(8,128)S(1)} %bitcast.14, f32[72,128]{1,0:T(8,128)S(1)} %get-tuple-element.12.gram_ref, f32[72,128]{1,0:T(8,128)S(1)} %get-tuple-element.13.rsum_ref, f32[128,128]{1,0:T(8,128)S(1)} %get-tuple-element.14.own_ref, ...), custom_call_target="tpu_custom_call" | custom-call | tf_op jit(solution)/shard_map/pallas_call | solution.py:299
  30.1 14.6 %all_to_all.20 = f32[32,1,768]{2,1,0:T(1,128)S(1)} all-to-all(f32[32,1,768]{2,1,0:T(1,128)S(1)} %bitcast.17), channel_id=1, replica_groups=mesh['x'=4,'y'=4,'h'=2,'z'=8,'c'=2] {'x','y','c'}, dimensions={0} | all-to-all | bytes 196608 | tf_op jit(solution)/shard_map/all_to_all | solution.py:334
  44.7 0.1 reduce_sum.20
  44.8 0.1 broadcast_in_dim.14
  44.9 19.6 %all_to_all.21 = f32[16,1,2944]{2,1,0:T(1,128)S(1)} all-to-all(f32[16,1,2944]{2,1,0:T(1,128)S(1)} %broadcast_in_dim.14), channel_id=1, replica_groups=mesh['x'=4,'y'=4,'h'=2,'z'=8,'c'=2] {'h','z'}, dimensions={0} | all-to-all | bytes 376832 | tf_op jit(solution)/shard_map/all_to_all | solution.py:334
  64.5 5.9 %collective-permute-start = (f32[16,1,2944]{2,1,0:T(1,128)S(1)}, f32[16,1,2944]{2,1,0:T(1,128)S(1)}, u32[]{:S(2)}, u32[]{:S(2)}) collective-permute-start(f32[16,1,2944]{2,1,0:T(1,128)S(1)} %all_to_all.21), channel_id=1, source_target_pairs={{0,1},{1,0},{2,3},{3,2},{4,5},{5,4},{6,7},{7,6},{8,9},{9,8},{10,11... | collective-permute-start | bytes 565256 | tf_op jit(solution)/shard_map/ppermute | solution.py:346
  70.5 0.1 broadcast_in_dim.15
  70.6 10.7 %all_to_all.22 = f32[32,1,768]{2,1,0:T(1,128)S(1)} all-to-all(f32[32,1,768]{2,1,0:T(1,128)S(1)} %broadcast_in_dim.15), channel_id=1, replica_groups=mesh['x'=4,'y'=4,'h'=2,'z'=8,'c'=2] {'x','y','c'}, dimensions={0} | all-to-all | bytes 196608 | tf_op jit(solution)/shard_map/all_to_all | solution.py:334
  81.3 0.0 collective-permute-done
  81.3 5.6 %shard_map.53 = (f32[1,64]{1,0:T(1,128)}, f32[8,512]{1,0:T(8,128)}) custom-call(f32[2080,128]{1,0:T(8,128)} %bitcast.20, f32[192,128]{1,0:T(8,128)S(1)} %bitcast.15, f32[368,128]{1,0:T(8,128)S(1)} %bitcast.13, f32[368,128]{1,0:T(8,128)S(1)} %bitcast.16, f32[128,512]{1,0:T(8,128)S(1)} %get-tuple-element.18.mask_ref, f32[8,512]{1,0:T(8,128)S(1)} %get-tuple-element.19.count_ref), custom_call_target="tpu_custom_call" | custom-call | tf_op jit(solution)/shard_map/pallas_call | solution.py:299
  (3 shorter events, 0.1 us)
Async XLA Ops:
  2.9 26.3 %all-to-all-start = ((f32[16,1,2176]{2,1,0:T(1,128)}), f32[16,1,2176]{2,1,0:T(1,128)S(1)}, u32[]{:S(2)}, u32[]{:S(2)}) async-start(f32[16,1,2176]{2,1,0:T(1,128)} %bitcast.5), calls=%async_computation | async-start | bytes 278528 | tf_op jit(solution)/shard_map/all_to_all | solution.py:334
  64.5 16.8 %collective-permute-start = (f32[16,1,2944]{2,1,0:T(1,128)S(1)}, f32[16,1,2944]{2,1,0:T(1,128)S(1)}, u32[]{:S(2)}, u32[]{:S(2)}) collective-permute-start(f32[16,1,2944]{2,1,0:T(1,128)S(1)} %all_to_all.21), channel_id=1, source_target_pairs={{0,1},{1,0},{2,3},{3,2},{4,5},{5,4},{6,7},{7,6},{8,9},{9,8},{10,11... | collective-permute-start | bytes 565256 | tf_op jit(solution)/shard_map/ppermute | solution.py:346

commit v6 on v4

--- a/solution.py
+++ b/solution.py
@@ -20,6 +20,13 @@
     return lax.dot_general(
         a, b, (((1,), (1,)), ((), ())), precision=HIGHEST, preferred_element_type=F32
     )
+
+
+def thirds(a):
+    high = a.astype(jnp.bfloat16).astype(F32)
+    rest = a - high
+    mid = rest.astype(jnp.bfloat16).astype(F32)
+    return [high, mid, rest - mid]
 
 
 def dot(a, b):
@@ -150,7 +157,12 @@
         cells = jnp.where(block == 4 * j + group, own, 0.0)
         weight = jnp.sum(cells, axis=0, keepdims=True)
         gram = gram + dot_t(spread * weight, spread)
-        rsum = rsum + dot_t(spread, cells)
+        three = jnp.concatenate(thirds(spread) + [jnp.zeros((8, 128), F32)], axis=0)
+        sums = lax.dot_general(
+            three.astype(jnp.bfloat16), cells.astype(jnp.bfloat16), (((1,), (1,)), ((), ())),
+            preferred_element_type=F32,
+        )
+        rsum = rsum + (sums[0:72] + sums[72:144] + sums[144:216])
     wide = jnp.concatenate([gram, jnp.zeros((ROWS, 128 - ROWS), F32)], axis=1)
     ret, rhs, row = rsum[64:72], wide[64:72], iota((8, 128), 0)
     extra = jnp.where(
@@ -250,7 +262,11 @@
     e = d1 + d2
     ew = jnp.sum(w * e, axis=0, keepdims=True)
     dw = jnp.sum(w * (e + d3), axis=0, keepdims=True)
-    back = dot(jnp.broadcast_to(ew, (8, 128)), mask_ref[...])[0:1]
+    back = lax.dot_general(
+        jnp.concatenate(thirds(ew) + [jnp.zeros((13, 128), F32)], axis=0).astype(jnp.bfloat16),
+        mask_ref[...].astype(jnp.bfloat16), (((1,), (0,)), ((), ())), preferred_element_type=F32,
+    )
+    back = back[0:1] + back[1:2] + back[2:3]
     here = iota((8, 128), 1) == 8 * day + iota((8, 128), 0)
     dw = jnp.sum(jnp.where(here, dw, 0.0), axis=1, keepdims=True)
     packed = jnp.zeros((16, 128), F32)

time: 87.3 us -> 87.9 us (level)
  no operation moved by 1% of the time
where the time goes in v6:
time: 87.9 us; the launch traced here: 87.5 us
  blocking collectives  34.2 us (39%)
  starting transfers between devices  23.6 us (27%)
  waiting for transfers between devices  16.4 us (19%)
  Pallas kernels  11.7 us (13%)
    all_to_all x2, blocking collectives, exchange(): return lax.all_to_all(x, axes, 0, 0, tiled=True)  34.2 us
    all_to_all x2, starting transfers between devices, exchange(): return lax.all_to_all(x, axes, 0, 0, tiled=True)  17.7 us
    all_to_all x2, waiting for transfers between devices, exchange(): return lax.all_to_all(x, axes, 0, 0, tiled=True)  16.4 us
    pallas_call x4, Pallas kernels, call(): pl.pallas_call(kernel, out_shape=[pltpu.VMEM(s, F32) if v else jax.ShapeD...  11.7 us
    ppermute x1, starting transfers between devices, on_device(): far = lax.ppermute(near, 'c', ((0, 1), (1, 0)))  5.95 us
  transfers between devices with their start and end apart: 3, of which 2 were waited for; matrix products, arithmetic and copies ran while one was open for 1% of the time, Pallas kernels for 4%

profile of v6, /device:TPU:1, one launch (start us, length us, event | category | flops | bytes accessed | tf_op | source)
XLA Modules:
  0.0 87.5 jit_solution(18053637574738783496)
XLA Ops:
  0.6 2.3 %shard_map.50 = f32[272,128]{1,0:T(8,128)} custom-call(s32[1]{0:T(128)} %bitcast.day_ref, f32[2080,128]{1,0:T(8,128)} %bitcast.20, s32[128,512]{1,0:T(8,128)} %pres_ref.1), custom_call_target="tpu_custom_call" | custom-call | tf_op jit(solution)/shard_map/pallas_call | solution.py:311
  2.9 14.0 %all-to-all-start = ((f32[16,1,2176]{2,1,0:T(1,128)}), f32[16,1,2176]{2,1,0:T(1,128)S(1)}, u32[]{:S(2)}, u32[]{:S(2)}) async-start(f32[16,1,2176]{2,1,0:T(1,128)} %bitcast.7), calls=%async_computation | async-start | bytes 278528 | tf_op jit(solution)/shard_map/all_to_all | solution.py:346
  16.9 3.3 %shard_map.51 = (f32[72,128]{1,0:T(8,128)S(1)}, f32[72,128]{1,0:T(8,128)S(1)}, f32[128,128]{1,0:T(8,128)S(1)}, f32[128,128]{1,0:T(8,128)S(1)}, f32[128,512]{1,0:T(8,128)S(1)}, /*index=5*/f32[8,512]{1,0:T(8,128)S(1)}) custom-call(s32[1]{0:T(128)} %bitcast.day_ref, f32[2080,128]{1,0:T(8,128)} %bitcast.21, s32[128,512]{1,0:T(8,128)} %pres_ref.1, s32[1,128]{1,0:T(1,128)} %bitcast.23), custom_call_target="tpu_custom_call" | custom-call | tf_op jit(solution)/shard_map/pallas_call | solution.py:311
  20.2 9.0 %all-to-all-done = f32[16,1,2176]{2,1,0:T(1,128)S(1)} async-done(((f32[16,1,2176]{2,1,0:T(1,128)}), f32[16,1,2176]{2,1,0:T(1,128)S(1)}, u32[]{:S(2)}, u32[]{:S(2)}) %all-to-all-start) | async-done | bytes 139296 | tf_op jit(solution)/shard_map/all_to_all | solution.py:346
  29.2 0.7 shard_map.52
  29.8 14.5 %all_to_all.20 = f32[32,1,768]{2,1,0:T(1,128)S(1)} all-to-all(f32[32,1,768]{2,1,0:T(1,128)S(1)} %bitcast.19), channel_id=1, replica_groups=mesh['x'=4,'y'=4,'h'=2,'z'=8,'c'=2] {'x','y','c'}, dimensions={0} | all-to-all | bytes 196608 | tf_op jit(solution)/shard_map/all_to_all | solution.py:346
  44.4 0.1 reduce_sum.20
  44.5 0.1 broadcast_in_dim.14
  44.6 19.6 %all_to_all.21 = f32[16,1,2944]{2,1,0:T(1,128)S(1)} all-to-all(f32[16,1,2944]{2,1,0:T(1,128)S(1)} %broadcast_in_dim.14), channel_id=1, replica_groups=mesh['x'=4,'y'=4,'h'=2,'z'=8,'c'=2] {'h','z'}, dimensions={0} | all-to-all | bytes 376832 | tf_op jit(solution)/shard_map/all_to_all | solution.py:346
  64.2 5.9 %collective-permute-start = (f32[16,1,2944]{2,1,0:T(1,128)S(1)}, f32[16,1,2944]{2,1,0:T(1,128)S(1)}, u32[]{:S(2)}, u32[]{:S(2)}) collective-permute-start(f32[16,1,2944]{2,1,0:T(1,128)S(1)} %all_to_all.21), channel_id=1, source_target_pairs={{0,1},{1,0},{2,3},{3,2},{4,5},{5,4},{6,7},{7,6},{8,9},{9,8},{10,11... | collective-permute-start | bytes 565256 | tf_op jit(solution)/shard_map/ppermute | solution.py:360
  70.2 0.7 broadcast_in_dim.15
  70.9 3.6 %all-to-all-start.3 = ((f32[32,1,768]{2,1,0:T(1,128)}), f32[32,1,768]{2,1,0:T(1,128)S(1)}, u32[]{:S(2)}, u32[]{:S(2)}) async-start(f32[32,1,768]{2,1,0:T(1,128)} %broadcast_in_dim.15), calls=%async_computation.3 | async-start | bytes 196608 | tf_op jit(solution)/shard_map/all_to_all | solution.py:346
  74.6 7.4 %all-to-all-done.3 = f32[32,1,768]{2,1,0:T(1,128)S(1)} async-done(((f32[32,1,768]{2,1,0:T(1,128)}), f32[32,1,768]{2,1,0:T(1,128)S(1)}, u32[]{:S(2)}, u32[]{:S(2)}) %all-to-all-start.3) | async-done | bytes 98336 | tf_op jit(solution)/shard_map/all_to_all | solution.py:346
  82.0 0.0 collective-permute-done
  82.0 5.5 %shard_map.53 = (f32[1,64]{1,0:T(1,128)}, f32[8,512]{1,0:T(8,128)}) custom-call(s32[1]{0:T(128)} %bitcast.day_ref, s32[1]{0:T(128)} %bitcast.1.side_ref, f32[2080,128]{1,0:T(8,128)} %bitcast.22, f32[192,128]{1,0:T(8,128)S(1)} %bitcast.17, f32[368,128]{1,0:T(8,128)S(1)} %bitcast.15, f32[368,128]{1,0:T(8,128)S(1)} %bitcast.18, ...), custom_call_target="tpu_custom_call" | custom-call | tf_op jit(solution)/shard_map/pallas_call | solution.py:311
  (3 shorter events, 0.1 us)
Async XLA Ops:
  2.9 26.3 %all-to-all-start = ((f32[16,1,2176]{2,1,0:T(1,128)}), f32[16,1,2176]{2,1,0:T(1,128)S(1)}, u32[]{:S(2)}, u32[]{:S(2)}) async-start(f32[16,1,2176]{2,1,0:T(1,128)} %bitcast.7), calls=%async_computation | async-start | bytes 278528 | tf_op jit(solution)/shard_map/all_to_all | solution.py:346
  64.2 17.8 %collective-permute-start = (f32[16,1,2944]{2,1,0:T(1,128)S(1)}, f32[16,1,2944]{2,1,0:T(1,128)S(1)}, u32[]{:S(2)}, u32[]{:S(2)}) collective-permute-start(f32[16,1,2944]{2,1,0:T(1,128)S(1)} %all_to_all.21), channel_id=1, source_target_pairs={{0,1},{1,0},{2,3},{3,2},{4,5},{5,4},{6,7},{7,6},{8,9},{9,8},{10,11... | collective-permute-start | bytes 565256 | tf_op jit(solution)/shard_map/ppermute | solution.py:360
  70.9 11.1 %all-to-all-start.3 = ((f32[32,1,768]{2,1,0:T(1,128)}), f32[32,1,768]{2,1,0:T(1,128)S(1)}, u32[]{:S(2)}, u32[]{:S(2)}) async-start(f32[32,1,768]{2,1,0:T(1,128)} %broadcast_in_dim.15), calls=%async_computation.3 | async-start | bytes 196608 | tf_op jit(solution)/shard_map/all_to_all | solution.py:346

commit v7 on v6

--- a/solution.py
+++ b/solution.py
@@ -262,11 +262,7 @@
     e = d1 + d2
     ew = jnp.sum(w * e, axis=0, keepdims=True)
     dw = jnp.sum(w * (e + d3), axis=0, keepdims=True)
-    back = lax.dot_general(
-        jnp.concatenate(thirds(ew) + [jnp.zeros((13, 128), F32)], axis=0).astype(jnp.bfloat16),
-        mask_ref[...].astype(jnp.bfloat16), (((1,), (0,)), ((), ())), preferred_element_type=F32,
-    )
-    back = back[0:1] + back[1:2] + back[2:3]
+    back = dot(jnp.broadcast_to(ew, (8, 128)), mask_ref[...])[0:1]
     here = iota((8, 128), 1) == 8 * day + iota((8, 128), 0)
     dw = jnp.sum(jnp.where(here, dw, 0.0), axis=1, keepdims=True)
     packed = jnp.zeros((16, 128), F32)

time: 87.9 us -> 87 us (0.990)
  Pallas kernels: 11.7 us -> 10.7 us
    pallas_call x4, Pallas kernels: 11.7 us -> 10.7 us  [call(): pl.pallas_call(kernel, out_shape=[pltpu.VMEM(s, F32) if v else jax.ShapeD...]
where the time goes in v7:
time: 87 us; the launch traced here: 86.5 us
  blocking collectives  34.2 us (39%)
  starting transfers between devices  23.6 us (27%)
  waiting for transfers between devices  16.4 us (19%)
  Pallas kernels  10.7 us (12%)
    all_to_all x2, blocking collectives, exchange(): return lax.all_to_all(x, axes, 0, 0, tiled=True)  34.2 us
    all_to_all x2, starting transfers between devices, exchange(): return lax.all_to_all(x, axes, 0, 0, tiled=True)  17.7 us
    all_to_all x2, waiting for transfers between devices, exchange(): return lax.all_to_all(x, axes, 0, 0, tiled=True)  16.4 us
    pallas_call x4, Pallas kernels, call(): pl.pallas_call(kernel, out_shape=[pltpu.VMEM(s, F32) if v else jax.ShapeD...  10.7 us
    ppermute x1, starting transfers between devices, on_device(): far = lax.ppermute(near, 'c', ((0, 1), (1, 0)))  5.95 us
  transfers between devices with their start and end apart: 3, of which 2 were waited for; matrix products, arithmetic and copies ran while one was open for 1% of the time, Pallas kernels for 4%

profile of v7, /device:TPU:1, one launch (start us, length us, event | category | flops | bytes accessed | tf_op | source)
XLA Modules:
  0.0 86.5 jit_solution(14025675275422127224)
XLA Ops:
  0.6 2.3 %shard_map.50 = f32[272,128]{1,0:T(8,128)} custom-call(s32[1]{0:T(128)} %bitcast.day_ref, f32[2080,128]{1,0:T(8,128)} %bitcast.20, s32[128,512]{1,0:T(8,128)} %pres_ref.1), custom_call_target="tpu_custom_call" | custom-call | tf_op jit(solution)/shard_map/pallas_call | solution.py:307
  2.9 14.0 %all-to-all-start = ((f32[16,1,2176]{2,1,0:T(1,128)}), f32[16,1,2176]{2,1,0:T(1,128)S(1)}, u32[]{:S(2)}, u32[]{:S(2)}) async-start(f32[16,1,2176]{2,1,0:T(1,128)} %bitcast.7), calls=%async_computation | async-start | bytes 278528 | tf_op jit(solution)/shard_map/all_to_all | solution.py:342
  16.9 3.3 %shard_map.51 = (f32[72,128]{1,0:T(8,128)S(1)}, f32[72,128]{1,0:T(8,128)S(1)}, f32[128,128]{1,0:T(8,128)S(1)}, f32[128,128]{1,0:T(8,128)S(1)}, f32[128,512]{1,0:T(8,128)S(1)}, /*index=5*/f32[8,512]{1,0:T(8,128)S(1)}) custom-call(s32[1]{0:T(128)} %bitcast.day_ref, f32[2080,128]{1,0:T(8,128)} %bitcast.21, s32[128,512]{1,0:T(8,128)} %pres_ref.1, s32[1,128]{1,0:T(1,128)} %bitcast.23), custom_call_target="tpu_custom_call" | custom-call | tf_op jit(solution)/shard_map/pallas_call | solution.py:307
  20.2 9.0 %all-to-all-done = f32[16,1,2176]{2,1,0:T(1,128)S(1)} async-done(((f32[16,1,2176]{2,1,0:T(1,128)}), f32[16,1,2176]{2,1,0:T(1,128)S(1)}, u32[]{:S(2)}, u32[]{:S(2)}) %all-to-all-start) | async-done | bytes 139296 | tf_op jit(solution)/shard_map/all_to_all | solution.py:342
  29.2 0.7 shard_map.52
  29.8 14.5 %all_to_all.20 = f32[32,1,768]{2,1,0:T(1,128)S(1)} all-to-all(f32[32,1,768]{2,1,0:T(1,128)S(1)} %bitcast.19), channel_id=1, replica_groups=mesh['x'=4,'y'=4,'h'=2,'z'=8,'c'=2] {'x','y','c'}, dimensions={0} | all-to-all | bytes 196608 | tf_op jit(solution)/shard_map/all_to_all | solution.py:342
  44.4 0.1 reduce_sum.20
  44.5 0.1 broadcast_in_dim.14
  44.6 19.6 %all_to_all.21 = f32[16,1,2944]{2,1,0:T(1,128)S(1)} all-to-all(f32[16,1,2944]{2,1,0:T(1,128)S(1)} %broadcast_in_dim.14), channel_id=1, replica_groups=mesh['x'=4,'y'=4,'h'=2,'z'=8,'c'=2] {'h','z'}, dimensions={0} | all-to-all | bytes 376832 | tf_op jit(solution)/shard_map/all_to_all | solution.py:342
  64.2 5.9 %collective-permute-start = (f32[16,1,2944]{2,1,0:T(1,128)S(1)}, f32[16,1,2944]{2,1,0:T(1,128)S(1)}, u32[]{:S(2)}, u32[]{:S(2)}) collective-permute-start(f32[16,1,2944]{2,1,0:T(1,128)S(1)} %all_to_all.21), channel_id=1, source_target_pairs={{0,1},{1,0},{2,3},{3,2},{4,5},{5,4},{6,7},{7,6},{8,9},{9,8},{10,11... | collective-permute-start | bytes 565256 | tf_op jit(solution)/shard_map/ppermute | solution.py:356
  70.2 0.7 broadcast_in_dim.15
  70.9 3.6 %all-to-all-start.3 = ((f32[32,1,768]{2,1,0:T(1,128)}), f32[32,1,768]{2,1,0:T(1,128)S(1)}, u32[]{:S(2)}, u32[]{:S(2)}) async-start(f32[32,1,768]{2,1,0:T(1,128)} %broadcast_in_dim.15), calls=%async_computation.3 | async-start | bytes 196608 | tf_op jit(solution)/shard_map/all_to_all | solution.py:342
  74.6 7.4 %all-to-all-done.3 = f32[32,1,768]{2,1,0:T(1,128)S(1)} async-done(((f32[32,1,768]{2,1,0:T(1,128)}), f32[32,1,768]{2,1,0:T(1,128)S(1)}, u32[]{:S(2)}, u32[]{:S(2)}) %all-to-all-start.3) | async-done | bytes 98336 | tf_op jit(solution)/shard_map/all_to_all | solution.py:342
  82.0 0.0 collective-permute-done
  82.0 4.5 %shard_map.53 = (f32[1,64]{1,0:T(1,128)}, f32[8,512]{1,0:T(8,128)}) custom-call(s32[1]{0:T(128)} %bitcast.day_ref, s32[1]{0:T(128)} %bitcast.1.side_ref, f32[2080,128]{1,0:T(8,128)} %bitcast.22, f32[192,128]{1,0:T(8,128)S(1)} %bitcast.17, f32[368,128]{1,0:T(8,128)S(1)} %bitcast.15, f32[368,128]{1,0:T(8,128)S(1)} %bitcast.18, ...), custom_call_target="tpu_custom_call" | custom-call | tf_op jit(solution)/shard_map/pallas_call | solution.py:307
  (3 shorter events, 0.1 us)
Async XLA Ops:
  2.9 26.3 %all-to-all-start = ((f32[16,1,2176]{2,1,0:T(1,128)}), f32[16,1,2176]{2,1,0:T(1,128)S(1)}, u32[]{:S(2)}, u32[]{:S(2)}) async-start(f32[16,1,2176]{2,1,0:T(1,128)} %bitcast.7), calls=%async_computation | async-start | bytes 278528 | tf_op jit(solution)/shard_map/all_to_all | solution.py:342
  64.2 17.8 %collective-permute-start = (f32[16,1,2944]{2,1,0:T(1,128)S(1)}, f32[16,1,2944]{2,1,0:T(1,128)S(1)}, u32[]{:S(2)}, u32[]{:S(2)}) collective-permute-start(f32[16,1,2944]{2,1,0:T(1,128)S(1)} %all_to_all.21), channel_id=1, source_target_pairs={{0,1},{1,0},{2,3},{3,2},{4,5},{5,4},{6,7},{7,6},{8,9},{9,8},{10,11... | collective-permute-start | bytes 565256 | tf_op jit(solution)/shard_map/ppermute | solution.py:356
  70.9 11.1 %all-to-all-start.3 = ((f32[32,1,768]{2,1,0:T(1,128)}), f32[32,1,768]{2,1,0:T(1,128)S(1)}, u32[]{:S(2)}, u32[]{:S(2)}) async-start(f32[32,1,768]{2,1,0:T(1,128)} %broadcast_in_dim.15), calls=%async_computation.3 | async-start | bytes 196608 | tf_op jit(solution)/shard_map/all_to_all | solution.py:342
